TPU v7x, 32 devices: a whole 2x2x4 slice. The times are simulated.
32 devices in a mesh: dp: 8 (over y, x, core), tensor: 4 (over z).
Axes of the slice: x: 2, y: 2, z: 4, core: 2. Of those that a mesh axis runs over, the one named last changes fastest.
Arguments:
- tokens: bfloat16 [16384, 1024], P(('dp', 'tensor')), may hold values from -6 to 6
- lengths: int32 [16], P('dp'), may hold values from 256 to 1024, as said below
- starts: int32 [16], P('dp'), may hold values from 0 to 768, as said below
- norm_one: float32 [1024], replicated, may hold values from 0.1 to 1.9
- w_query: bfloat16 [1024, 1024], P('dp', 'tensor'), may hold values from -0.1875 to 0.1875
- w_key: bfloat16 [1024, 1024], P('dp', 'tensor'), may hold values from -0.1875 to 0.1875
- w_value: bfloat16 [1024, 2048], P('dp', 'tensor'), may hold values from -0.1875 to 0.1875
- w_gating: bfloat16 [1024, 2048], P('dp', 'tensor'), may hold values from -0.1875 to 0.1875
- w_decay: bfloat16 [1024, 8], P('dp', 'tensor'), may hold values from -0.1875 to 0.1875
- w_strength: bfloat16 [1024, 8], P('dp', 'tensor'), may hold values from -0.1875 to 0.1875
- filter_query: float32 [4, 1024], replicated, may hold values from -3 to 3
- filter_key: float32 [4, 1024], replicated, may hold values from -3 to 3
- filter_value: float32 [4, 2048], replicated, may hold values from -3 to 3
- decay_log: float32 [8], replicated, may hold values from -1 to 2.5
- decay_bias: float32 [8], replicated, may hold values from -6 to -1
- head_gain: float32 [256], replicated, may hold values from 0.1 to 1.9
- w_output: bfloat16 [2048, 1024], P('tensor', 'dp'), may hold values from -0.25 to 0.25
- norm_two: float32 [1024], replicated, may hold values from 0.1 to 1.9
- w_gate: bfloat16 [1024, 2816], P('dp', 'tensor'), may hold values from -0.1875 to 0.1875
- w_up: bfloat16 [1024, 2816], P('dp', 'tensor'), may hold values from -0.1875 to 0.1875
- w_down: bfloat16 [2816, 1024], P('tensor', 'dp'), may hold values from -0.15625 to 0.15625
- cotangent: bfloat16 [16384, 1024], P(('dp', 'tensor')), may hold values from -6 to 6
Outputs:
- block_out: bfloat16 [16384, 1024], P(('dp', 'tensor'))
- grad_tokens: float32 [16384, 1024], P(('dp', 'tensor'))
- grad_norm_one: float32 [1024], replicated
- grad_w_query: float32 [1024, 1024], P('dp', 'tensor')
- grad_w_key: float32 [1024, 1024], P('dp', 'tensor')
- grad_w_value: float32 [1024, 2048], P('dp', 'tensor')
- grad_w_gating: float32 [1024, 2048], P('dp', 'tensor')
- grad_w_decay: float32 [1024, 8], P('dp', 'tensor')
- grad_w_strength: float32 [1024, 8], P('dp', 'tensor')
- grad_filter_query: float32 [4, 1024], replicated
- grad_filter_key: float32 [4, 1024], replicated
- grad_filter_value: float32 [4, 2048], replicated
- grad_decay_log: float32 [8], replicated
- grad_decay_bias: float32 [8], replicated
- grad_head_gain: float32 [256], replicated
- grad_w_output: float32 [2048, 1024], P('tensor', 'dp')
- grad_norm_two: float32 [1024], replicated
- grad_w_gate: float32 [1024, 2816], P('dp', 'tensor')
- grad_w_up: float32 [1024, 2816], P('dp', 'tensor')
- grad_w_down: float32 [2816, 1024], P('tensor', 'dp')
Inputs may be any that keep to these rules, and one draw needn't show every extreme that they name: lengths[0] = 1024 and lengths[1] = 256. starts[r] + lengths[r] <= 1024; starts[1] = 768.
All inputs are finite; a program needn't handle non-finite values.
Results may differ from a plain program's by a relative error of at most 0.013.
Values may be sent and summed in bfloat16 or wider, within the bound.
No kernel may reach another device: no remote copies, remote signals or barrier semaphores. Data moves between devices by JAX's collectives and lax.ppermute only.
A program may use at most 256 MiB of HBM per device.

v0:
```python
import jax
import jax.numpy as jnp
from jax import lax
from jax.sharding import PartitionSpec as P

DK = 128
DV = 256
SPAN = 64
SLOT = 1024


def causal_filter(inputs, taps):
    length = inputs.shape[1]
    width = taps.shape[0]
    padded = jnp.pad(inputs, ((0, 0), (width - 1, 0), (0, 0)))
    total = jnp.zeros_like(inputs)
    for offset in range(width):
        total = total + taps[offset] * padded[:, offset : offset + length]
    return jax.nn.silu(total)


def unit_rows(values):
    return values * lax.rsqrt(jnp.sum(values * values, -1, keepdims=True) + 1e-06)


def span_rule(queries, keys, values, writes, decays):
    rows, heads, length, kdim = queries.shape
    vdim = values.shape[-1]
    count = length // SPAN
    highest = lax.Precision.HIGHEST

    def blocks(array):
        shaped = array.reshape((rows, heads, count, SPAN) + array.shape[3:])
        return jnp.moveaxis(shaped, 2, 0)

    strict = jnp.tril(jnp.ones((SPAN, SPAN), jnp.float32), -1)
    causal = jnp.tril(jnp.ones((SPAN, SPAN), jnp.float32))
    identity = jnp.eye(SPAN, dtype=jnp.float32)

    def advance(state, block):
        block_q, block_k, block_v, block_w, block_d = block
        cumulative = jnp.cumsum(block_d, -1)
        spread = jnp.exp(jnp.minimum(cumulative[..., :, None] - cumulative[..., None, :], 0.0))
        keys_keys = jnp.einsum("rhid,rhjd->rhij", block_k, block_k, precision=highest)
        system = identity + block_w[..., :, None] * spread * keys_keys * strict
        growth = jnp.exp(cumulative)
        source = block_w[..., None] * block_v - (block_w * growth)[..., None] * jnp.einsum(
            "rhid,rhde->rhie", block_k, state, precision=highest
        )
        delta = lax.linalg.triangular_solve(system, source, left_side=True, lower=True)
        scores = (
            jnp.einsum("rhid,rhjd->rhij", block_q, block_k, precision=highest) * spread * causal
        )
        emitted = growth[..., None] * jnp.einsum(
            "rhid,rhde->rhie", block_q, state, precision=highest
        )
        emitted = emitted + jnp.einsum("rhij,rhje->rhie", scores, delta, precision=highest)
        remain = jnp.exp(cumulative[..., -1:] - cumulative)
        new_state = jnp.exp(cumulative[..., -1])[..., None, None] * state
        new_state = new_state + jnp.einsum(
            "rhid,rhie->rhde", block_k * remain[..., None], delta, precision=highest
        )
        return (new_state, emitted)

    start_state = jnp.zeros((rows, heads, kdim, vdim), jnp.float32)
    _, outputs = lax.scan(
        jax.checkpoint(advance),
        start_state,
        (blocks(queries), blocks(keys), blocks(values), blocks(writes), blocks(decays)),
    )
    return jnp.moveaxis(outputs, 0, 2).reshape(rows, heads, length, vdim)


def mixing(
    proj_query,
    proj_key,
    proj_value,
    proj_gate,
    proj_decay,
    proj_strength,
    filter_query,
    filter_key,
    filter_value,
    decay_log,
    decay_bias,
    head_gain,
    row_mask,
):
    rows, length = row_mask.shape
    heads = proj_decay.shape[-1]
    valid = row_mask[..., None]
    queries = causal_filter(proj_query * valid, filter_query).reshape(rows, length, heads, DK)
    keys = causal_filter(proj_key * valid, filter_key).reshape(rows, length, heads, DK)
    values = causal_filter(proj_value * valid, filter_value).reshape(rows, length, heads, DV)
    queries = unit_rows(queries) * DK ** (-0.5)
    keys = unit_rows(keys) * valid[..., None]
    writes = jax.nn.sigmoid(proj_strength) * valid
    decays = -jnp.exp(decay_log) * jax.nn.softplus(proj_decay + decay_bias) * valid
    outputs = span_rule(
        jnp.moveaxis(queries, 2, 1),
        jnp.moveaxis(keys, 2, 1),
        jnp.moveaxis(values, 2, 1),
        jnp.moveaxis(writes, 2, 1),
        jnp.moveaxis(decays, 2, 1),
    )
    outputs = jnp.moveaxis(outputs, 1, 2)
    outputs = (
        outputs * lax.rsqrt(jnp.mean(outputs * outputs, -1, keepdims=True) + 1e-05) * head_gain
    )
    gating = jax.nn.silu(proj_gate).reshape(rows, length, heads, DV)
    return (outputs * gating * valid[..., None]).reshape(rows, length, heads * DV)


def inner_rows(left, right):
    return lax.dot_general(
        left, right, (((0,), (0,)), ((), ())), preferred_element_type=jnp.float32
    )


def times_transposed(left, right):
    return lax.dot_general(
        left, right, (((1,), (1,)), ((), ())), preferred_element_type=jnp.float32
    )


def norm_backward(grad_normed, inputs, scale, gain):
    unit = inputs * scale
    weighted = grad_normed * gain
    grad_gain = jnp.sum(grad_normed * unit, 0)
    grad_inputs = scale * (weighted - unit * jnp.mean(weighted * unit, -1, keepdims=True))
    return (grad_inputs, grad_gain)


def shards(
    tokens,
    lengths,
    starts,
    norm_one,
    w_query,
    w_key,
    w_value,
    w_gating,
    w_decay,
    w_strength,
    filter_query,
    filter_key,
    filter_value,
    decay_log,
    decay_bias,
    head_gain,
    w_output,
    norm_two,
    w_gate,
    w_up,
    w_down,
    cotangent,
):
    rank = lax.axis_index("tensor")
    tok_dev = tokens.shape[0]
    rows = lengths.shape[0]
    heads_local = w_decay.shape[1]
    slot_pos = jnp.arange(SLOT, dtype=jnp.int32)
    row_mask = (
        (slot_pos[None, :] >= starts[:, None]) & (slot_pos[None, :] < (starts + lengths)[:, None])
    ).astype(jnp.float32)
    local_mask = lax.dynamic_slice_in_dim(row_mask.reshape(-1), rank * tok_dev, tok_dev)[:, None]
    gathered = (
        lax.all_gather(w_query, "dp", axis=0, tiled=True),
        lax.all_gather(w_key, "dp", axis=0, tiled=True),
        lax.all_gather(w_value, "dp", axis=0, tiled=True),
        lax.all_gather(w_gating, "dp", axis=0, tiled=True),
        lax.all_gather(w_decay, "dp", axis=0, tiled=True),
        lax.all_gather(w_strength, "dp", axis=0, tiled=True),
        lax.all_gather(w_output, "dp", axis=1, tiled=True),
        lax.all_gather(w_gate, "dp", axis=0, tiled=True),
        lax.all_gather(w_up, "dp", axis=0, tiled=True),
        lax.all_gather(w_down, "dp", axis=1, tiled=True),
    )
    (
        full_query,
        full_key,
        full_value,
        full_gating,
        full_decay,
        full_strength,
        full_output,
        full_gate,
        full_up,
        full_down,
    ) = gathered
    inputs = tokens.astype(jnp.float32)
    scale_one = lax.rsqrt(jnp.mean(inputs * inputs, -1, keepdims=True) + 1e-05)
    normed_one = (inputs * scale_one * norm_one).astype(jnp.bfloat16)
    rows_one = lax.all_gather(normed_one, "tensor", axis=0, tiled=True)
    projections = tuple(
        (
            jnp.dot(rows_one, weight, preferred_element_type=jnp.float32).reshape(rows, SLOT, -1)
            for weight in (full_query, full_key, full_value, full_gating, full_decay, full_strength)
        )
    )
    key_width = heads_local * DK
    value_width = heads_local * DV
    local_params = (
        lax.dynamic_slice_in_dim(filter_query, rank * key_width, key_width, 1),
        lax.dynamic_slice_in_dim(filter_key, rank * key_width, key_width, 1),
        lax.dynamic_slice_in_dim(filter_value, rank * value_width, value_width, 1),
        lax.dynamic_slice_in_dim(decay_log, rank * heads_local, heads_local),
        lax.dynamic_slice_in_dim(decay_bias, rank * heads_local, heads_local),
        head_gain,
    )

    def local_mixing(*values):
        return mixing(*values, row_mask)

    mixed_float, pull_mixing = jax.vjp(local_mixing, *projections + local_params)
    mixed = mixed_float.reshape(rows * SLOT, -1).astype(jnp.bfloat16)
    attention = lax.psum_scatter(
        jnp.dot(mixed, full_output, preferred_element_type=jnp.float32),
        "tensor",
        scatter_dimension=0,
        tiled=True,
    )
    middle = inputs + attention
    scale_two = lax.rsqrt(jnp.mean(middle * middle, -1, keepdims=True) + 1e-05)
    normed_two = (middle * scale_two * norm_two).astype(jnp.bfloat16)
    rows_two = lax.all_gather(normed_two, "tensor", axis=0, tiled=True)
    gate_pre = jnp.dot(rows_two, full_gate, preferred_element_type=jnp.float32)
    up_pre = jnp.dot(rows_two, full_up, preferred_element_type=jnp.float32)
    hidden = (jax.nn.silu(gate_pre) * up_pre).astype(jnp.bfloat16)
    feed = lax.psum_scatter(
        jnp.dot(hidden, full_down, preferred_element_type=jnp.float32).astype(jnp.bfloat16),
        "tensor",
        scatter_dimension=0,
        tiled=True,
    ).astype(jnp.float32)
    block_out = (local_mask * (middle + feed)).astype(jnp.bfloat16)
    back_weights = (
        lax.all_gather(w_query, "dp", axis=0, tiled=True),
        lax.all_gather(w_key, "dp", axis=0, tiled=True),
        lax.all_gather(w_value, "dp", axis=0, tiled=True),
        lax.all_gather(w_gating, "dp", axis=0, tiled=True),
        lax.all_gather(w_decay, "dp", axis=0, tiled=True),
        lax.all_gather(w_strength, "dp", axis=0, tiled=True),
        lax.all_gather(w_output, "dp", axis=1, tiled=True),
        lax.all_gather(w_gate, "dp", axis=0, tiled=True),
        lax.all_gather(w_up, "dp", axis=0, tiled=True),
        lax.all_gather(w_down, "dp", axis=1, tiled=True),
    )
    (
        back_query,
        back_key,
        back_value,
        back_gating,
        back_decay,
        back_strength,
        back_output,
        back_gate,
        back_up,
        back_down,
    ) = back_weights
    residual_grad = cotangent.astype(jnp.float32) * local_mask
    feed_grad = lax.all_gather(residual_grad.astype(jnp.bfloat16), "tensor", axis=0, tiled=True)
    hidden_grad = times_transposed(feed_grad, back_down)
    grad_down = inner_rows(hidden, feed_grad)
    sigmoid_gate = jax.nn.sigmoid(gate_pre)
    gate_grad = (
        hidden_grad * up_pre * sigmoid_gate * (1.0 + gate_pre * (1.0 - sigmoid_gate))
    ).astype(jnp.bfloat16)
    up_grad = (hidden_grad * gate_pre * sigmoid_gate).astype(jnp.bfloat16)
    grad_gate = inner_rows(rows_two, gate_grad)
    grad_up = inner_rows(rows_two, up_grad)
    normed_two_grad = lax.psum_scatter(
        times_transposed(gate_grad, back_gate) + times_transposed(up_grad, back_up),
        "tensor",
        scatter_dimension=0,
        tiled=True,
    )
    middle_part, grad_norm_two = norm_backward(normed_two_grad, middle, scale_two, norm_two)
    middle_grad = residual_grad + middle_part
    attention_grad = lax.all_gather(middle_grad.astype(jnp.bfloat16), "tensor", axis=0, tiled=True)
    mixed_grad = times_transposed(attention_grad, back_output)
    grad_output = inner_rows(mixed, attention_grad)
    pulled = pull_mixing(mixed_grad.reshape(rows, SLOT, -1))
    projection_grads = tuple(
        (grad.reshape(rows * SLOT, -1).astype(jnp.bfloat16) for grad in pulled[:6])
    )
    weight_grads = tuple((inner_rows(rows_one, grad) for grad in projection_grads))
    back_projections = (back_query, back_key, back_value, back_gating, back_decay, back_strength)
    normed_one_part = times_transposed(projection_grads[0], back_projections[0])
    for grad, weight in zip(projection_grads[1:], back_projections[1:]):
        normed_one_part = normed_one_part + times_transposed(grad, weight)
    normed_one_grad = lax.psum_scatter(
        normed_one_part.astype(jnp.bfloat16), "tensor", scatter_dimension=0, tiled=True
    ).astype(jnp.float32)
    input_part, grad_norm_one = norm_backward(normed_one_grad, inputs, scale_one, norm_one)
    grad_tokens = middle_grad + input_part
    placed_query = lax.dynamic_update_slice_in_dim(
        jnp.zeros_like(filter_query), pulled[6], rank * key_width, 1
    )
    placed_key = lax.dynamic_update_slice_in_dim(
        jnp.zeros_like(filter_key), pulled[7], rank * key_width, 1
    )
    placed_value = lax.dynamic_update_slice_in_dim(
        jnp.zeros_like(filter_value), pulled[8], rank * value_width, 1
    )
    placed_log = lax.dynamic_update_slice_in_dim(
        jnp.zeros_like(decay_log), pulled[9], rank * heads_local, 0
    )
    placed_bias = lax.dynamic_update_slice_in_dim(
        jnp.zeros_like(decay_bias), pulled[10], rank * heads_local, 0
    )
    summed = lax.psum(
        (
            grad_norm_one,
            grad_norm_two,
            pulled[11],
            placed_query,
            placed_key,
            placed_value,
            placed_log,
            placed_bias,
        ),
        ("dp", "tensor"),
    )
    (
        sum_norm_one,
        sum_norm_two,
        sum_head_gain,
        sum_filter_query,
        sum_filter_key,
        sum_filter_value,
        sum_decay_log,
        sum_decay_bias,
    ) = summed
    (
        owned_query,
        owned_key,
        owned_value,
        owned_gating,
        owned_decay,
        owned_strength,
        owned_output,
        owned_gate,
        owned_up,
        owned_down,
    ) = (
        lax.psum_scatter(weight_grads[0], "dp", scatter_dimension=0, tiled=True),
        lax.psum_scatter(weight_grads[1], "dp", scatter_dimension=0, tiled=True),
        lax.psum_scatter(weight_grads[2], "dp", scatter_dimension=0, tiled=True),
        lax.psum_scatter(weight_grads[3], "dp", scatter_dimension=0, tiled=True),
        lax.psum_scatter(weight_grads[4], "dp", scatter_dimension=0, tiled=True),
        lax.psum_scatter(weight_grads[5], "dp", scatter_dimension=0, tiled=True),
        lax.psum_scatter(grad_output, "dp", scatter_dimension=1, tiled=True),
        lax.psum_scatter(grad_gate, "dp", scatter_dimension=0, tiled=True),
        lax.psum_scatter(grad_up, "dp", scatter_dimension=0, tiled=True),
        lax.psum_scatter(grad_down, "dp", scatter_dimension=1, tiled=True),
    )
    return (
        block_out,
        grad_tokens,
        sum_norm_one,
        owned_query,
        owned_key,
        owned_value,
        owned_gating,
        owned_decay,
        owned_strength,
        sum_filter_query,
        sum_filter_key,
        sum_filter_value,
        sum_decay_log,
        sum_decay_bias,
        sum_head_gain,
        owned_output,
        sum_norm_two,
        owned_gate,
        owned_up,
        owned_down,
    )


def solution(mesh):
    placed = (
        P(("dp", "tensor"), None),
        P("dp"),
        P("dp"),
        P(),
        P("dp", "tensor"),
        P("dp", "tensor"),
        P("dp", "tensor"),
        P("dp", "tensor"),
        P("dp", "tensor"),
        P("dp", "tensor"),
        P(),
        P(),
        P(),
        P(),
        P(),
        P(),
        P("tensor", "dp"),
        P(),
        P("dp", "tensor"),
        P("dp", "tensor"),
        P("tensor", "dp"),
        P(("dp", "tensor"), None),
    )
    return jax.shard_map(
        shards,
        mesh=mesh,
        in_specs=placed,
        out_specs=(
            P(("dp", "tensor"), None),
            P(("dp", "tensor"), None),
            P(),
            P("dp", "tensor"),
            P("dp", "tensor"),
            P("dp", "tensor"),
            P("dp", "tensor"),
            P("dp", "tensor"),
            P("dp", "tensor"),
            P(),
            P(),
            P(),
            P(),
            P(),
            P(),
            P("tensor", "dp"),
            P(),
            P("dp", "tensor"),
            P("dp", "tensor"),
            P("tensor", "dp"),
        ),
        check_vma=False,
    )
```

profile of v0, /device:TPU:8, one launch (start us, length us, event | category | flops | bytes accessed | tf_op | source)
XLA Modules:
  0.0 2799.9 jit_solution(7895488320774858217)
XLA Ops:
  53.0 37.8 %all-gather.11.cloned.1.call-done = bf16[2048,1024]{1,0:T(8,128)(2,1)} async-done(((bf16[512,1024]{1,0:T(8,128)(2,1)}), bf16[2048,1024]{1,0:T(8,128)(2,1)}) %all-gather.11.cloned.1.call-update) | async-done | bytes 4194320 | tf_op jit(solution)/shard_map/all_gather | solution.py:194
  165.2 492.0 %while.40 = (s32[]{:T(128)}, f32[2,2,128,256]{3,2,1,0:T(8,128)S(1)}, f32[16,2,2,64,256]{4,3,0,2,1:T(8,128)}, f32[16,2,2,128,256]{4,3,2,1,0:T(8,128)}, f32[16,2,2...) while((s32[]{:T(128)}, ...), condition=%wide.region_5.7_spmd.clone, body=%wide.region_3.6_spmd.clone.sunk | while | flops 454357248 | bytes 6743030 | solution.py:66
  168.1 19.7 custom-call.23
  229.6 19.7 custom-call.23
  260.3 19.7 custom-call.23
  687.7 145.1 %reduce-scatter.19.cloned.1.call-done = f32[512,1024]{1,0:T(8,128)} async-done(((f32[2048,1024]{1,0:T(8,128)}), f32[512,1024]{1,0:T(8,128)}) %reduce-scatter.19.cloned.1.call-update) | async-done | bytes 2097168 | tf_op jit(solution)/shard_map/reduce_scatter | solution.py:217
  839.0 21.8 all-gather.21.cloned.1.call-done
  860.8 80.2 %all-gather.19.cloned.1.call-done = bf16[2048,1024]{1,0:T(8,128)(2,1)} async-done(((bf16[512,1024]{1,0:T(8,128)(2,1)}), bf16[2048,1024]{1,0:T(8,128)(2,1)}) %all-gather.19.cloned.1.call-update) | async-done | bytes 4194320 | tf_op jit(solution)/shard_map/all_gather | solution.py:226
  949.4 19.9 all-gather.23.cloned.1.call-done
  996.4 79.5 %all-gather.27.cloned.1.call-done = bf16[2048,1024]{1,0:T(8,128)(2,1)} async-done(((bf16[512,1024]{1,0:T(8,128)(2,1)}), bf16[2048,1024]{1,0:T(8,128)(2,1)}) %all-gather.27.cloned.1.call-update) | async-done | bytes 4194320 | tf_op jit(solution)/shard_map/all_gather | solution.py:262
  1105.4 137.5 %reduce-scatter.23.cloned.1.call-done = f32[512,1024]{1,0:T(8,128)} async-done(((f32[2048,1024]{1,0:T(8,128)}), f32[512,1024]{1,0:T(8,128)}) %reduce-scatter.23.cloned.1.call-update) | async-done | bytes 2097168 | tf_op jit(solution)/shard_map/reduce_scatter | solution.py:272
  1245.7 77.2 %reduce-scatter.21.cloned.1.call-done = bf16[512,1024]{1,0:T(8,128)(2,1)} async-done(((bf16[2048,1024]{1,0:T(8,128)(2,1)}), bf16[512,1024]{1,0:T(8,128)(2,1)}) %reduce-scatter.21.cloned.1.call-update) | async-done | bytes 1048592 | tf_op jit(solution)/shard_map/reduce_scatter | solution.py:230
  1327.8 78.7 %all-gather.29.cloned.1.call-done = bf16[2048,1024]{1,0:T(8,128)(2,1)} async-done(((bf16[512,1024]{1,0:T(8,128)(2,1)}), bf16[2048,1024]{1,0:T(8,128)(2,1)}) %all-gather.29.cloned.1.call-update) | async-done | bytes 4194320 | tf_op jit(solution)/shard_map/all_gather | solution.py:280
  1436.4 626.9 %while.41 = (s32[]{:T(128)}, f32[2,2,128,256]{3,2,1,0:T(8,128)S(1)}, f32[16,2,2,64,128]{4,3,0,2,1:T(8,128)}, f32[16,2,2,64,128]{4,3,0,2,1:T(8,128)}, f32[16,2,2,...) while((s32[]{:T(128)}, ...), condition=%wide.region_25.27_spmd.clone, body=%wide.region_13.26_spmd.clone.sunk | while | flops 1223604480 | bytes 21116660 | solution.py:66
  2237.3 50.4 %reduce-scatter.25.cloned.1.call-done = bf16[512,1024]{1,0:T(8,128)(2,1)} async-done(((bf16[2048,1024]{1,0:T(8,128)(2,1)}), bf16[512,1024]{1,0:T(8,128)(2,1)}) %reduce-scatter.25.cloned.1.call-update) | async-done | bytes 1048592 | tf_op jit(solution)/shard_map/reduce_scatter | solution.py:292
  2293.6 43.2 %reduce-scatter.37.cloned.1.call-done = f32[128,704]{0,1:T(8,128)} async-done(((f32[1024,704]{0,1:T(8,128)}), f32[128,704]{0,1:T(8,128)}) %reduce-scatter.37.cloned.1.call-update) | async-done | bytes 360464 | tf_op jit(solution)/shard_map/reduce_scatter | solution.py:354
  2336.8 48.6 %reduce-scatter.39.cloned.1.call-done = f32[128,704]{0,1:T(8,128)} async-done(((f32[1024,704]{0,1:T(8,128)}), f32[128,704]{0,1:T(8,128)}) %reduce-scatter.39.cloned.1.call-update) | async-done | bytes 360464 | tf_op jit(solution)/shard_map/reduce_scatter | solution.py:355
  2385.4 48.7 %reduce-scatter.41.cloned.1.call-done = f32[704,128]{1,0:T(8,128)} async-done(((f32[704,1024]{1,0:T(8,128)}), f32[704,128]{1,0:T(8,128)}) %reduce-scatter.41.cloned.1.call-update) | async-done | bytes 360464 | tf_op jit(solution)/shard_map/reduce_scatter | solution.py:356
  2434.1 39.6 %reduce-scatter.27.cloned.1.call-done = f32[128,256]{1,0:T(8,128)} async-done(((f32[1024,256]{1,0:T(8,128)}), f32[128,256]{1,0:T(8,128)}) %reduce-scatter.27.cloned.1.call-update) | async-done | bytes 131088 | tf_op jit(solution)/shard_map/reduce_scatter | solution.py:347
  2473.7 39.8 %reduce-scatter.29.cloned.1.call-done = f32[128,256]{1,0:T(8,128)} async-done(((f32[1024,256]{1,0:T(8,128)}), f32[128,256]{1,0:T(8,128)}) %reduce-scatter.29.cloned.1.call-update) | async-done | bytes 131088 | tf_op jit(solution)/shard_map/reduce_scatter | solution.py:348
  2513.5 45.0 %reduce-scatter.35.cloned.1.call-done = f32[512,128]{1,0:T(8,128)} async-done(((f32[512,1024]{1,0:T(8,128)}), f32[512,128]{1,0:T(8,128)}) %reduce-scatter.35.cloned.1.call-update) | async-done | bytes 262160 | tf_op jit(solution)/shard_map/reduce_scatter | solution.py:353
  2558.5 45.0 %reduce-scatter.31.cloned.1.call-done = f32[128,512]{1,0:T(8,128)} async-done(((f32[1024,512]{1,0:T(8,128)}), f32[128,512]{1,0:T(8,128)}) %reduce-scatter.31.cloned.1.call-update) | async-done | bytes 262160 | tf_op jit(solution)/shard_map/reduce_scatter | solution.py:349
  2603.5 44.8 %reduce-scatter.33.cloned.1.call-done = f32[128,512]{1,0:T(8,128)} async-done(((f32[1024,512]{1,0:T(8,128)}), f32[128,512]{1,0:T(8,128)}) %reduce-scatter.33.cloned.1.call-update) | async-done | bytes 262160 | tf_op jit(solution)/shard_map/reduce_scatter | solution.py:350
  2648.3 134.5 %all-reduce.32.cloned.1.call-done = (f32[1024]{0:T(1024)}, f32[4,1024]{1,0:T(4,128)}, f32[4,1024]{1,0:T(4,128)}, f32[4,2048]{1,0:T(4,128)}, f32[8]{0:T(128)}, /*index=5*/f32[8]{0:T(128)}, f32[256]{0:T(256)}, f32[1024]{0:T(1024)}) async-done(((f32[1024]{0:T(1024)}, f32[4,1024]{1,0:T(4,128)}, f32[4,1024]{1,0:T(4,128)}, f32[4,2048]{1,0:T(4,128)}, f32[8]{0:T(128)}, /*index=5*/f32[8]{0:T(128)}, f32[256]{0:T(256)}, ...) | async-done | bytes 74832 | tf_op jit(solution)/shard_map/psum | solution.py:312
  (1399 shorter events, 1502.9 us)
Async XLA Ops:
  11.4 116.1 %all-gather.13.cloned.1.call-start = ((), (), s32[]{:S(2)}) async-start(), calls=%async_computation.15 | async-start | bytes 1179648 | tf_op jit(solution)/shard_map/all_gather | solution.py:170
  12.2 645.1 %all-gather.15.cloned.1.call-start = ((), (), s32[]{:S(2)}) async-start(), calls=%async_computation.16 | async-start | bytes 1179648 | tf_op jit(solution)/shard_map/all_gather | solution.py:171
  12.9 666.6 %all-gather.17.cloned.1.call-start = ((), (), s32[]{:S(2)}) async-start(), calls=%async_computation.17 | async-start | bytes 1179648 | tf_op jit(solution)/shard_map/all_gather | solution.py:174
  13.5 819.3 %reduce-scatter.19.cloned.1.call-start = ((), (), s32[]{:S(2)}) async-start(), calls=%async_computation.18 | async-start | bytes 10485760 | tf_op jit(solution)/shard_map/reduce_scatter | solution.py:217
  687.1 173.7 %all-gather.21.cloned.1.call-start = ((), (), s32[]{:S(2)}) async-start(), calls=%async_computation.20 | async-start | bytes 1622016 | tf_op jit(solution)/shard_map/all_gather | solution.py:175
  687.7 253.4 %all-gather.19.cloned.1.call-start = ((), (), s32[]{:S(2)}) async-start(), calls=%async_computation.19 | async-start | bytes 5242880 | tf_op jit(solution)/shard_map/all_gather | solution.py:226
  836.0 133.3 %all-gather.23.cloned.1.call-start = ((), (), s32[]{:S(2)}) async-start(), calls=%async_computation.21 | async-start | bytes 1622016 | tf_op jit(solution)/shard_map/all_gather | solution.py:176
  836.8 159.7 %all-gather.25.cloned.1.call-start = ((), (), s32[]{:S(2)}) async-start(), calls=%async_computation.22 | async-start | bytes 1622016 | tf_op jit(solution)/shard_map/all_gather | solution.py:177
  837.5 238.5 %all-gather.27.cloned.1.call-start = ((), (), s32[]{:S(2)}) async-start(), calls=%async_computation.24 | async-start | bytes 5242880 | tf_op jit(solution)/shard_map/all_gather | solution.py:262
  838.9 404.0 %reduce-scatter.23.cloned.1.call-start = ((), (), s32[]{:S(2)}) async-start(), calls=%async_computation.25 | async-start | bytes 10485760 | tf_op jit(solution)/shard_map/reduce_scatter | solution.py:272
  1097.4 225.5 %reduce-scatter.21.cloned.1.call-start = ((), (), s32[]{:S(2)}) async-start(), calls=%async_computation.23 | async-start | bytes 5242880 | tf_op jit(solution)/shard_map/reduce_scatter | solution.py:230
  1105.2 301.2 %all-gather.29.cloned.1.call-start = ((), (), s32[]{:S(2)}) async-start(), calls=%async_computation.26 | async-start | bytes 5242880 | tf_op jit(solution)/shard_map/all_gather | solution.py:280
  1327.7 906.5 %reduce-scatter.43.cloned.1.call-start = ((), (), s32[]{:S(2)}) async-start(), calls=%async_computation.36 | async-start | bytes 589824
  2136.3 99.6 %reduce-scatter.45.cloned.1.call-start = ((), (), s32[]{:S(2)}) async-start(), calls=%async_computation.37 | async-start | bytes 589824
  2151.0 136.8 %reduce-scatter.25.cloned.1.call-start = ((), (), s32[]{:S(2)}) async-start(), calls=%async_computation.27 | async-start | bytes 5242880 | tf_op jit(solution)/shard_map/reduce_scatter | solution.py:292
  2181.0 155.8 %reduce-scatter.37.cloned.1.call-start = ((), (), s32[]{:S(2)}) async-start(), calls=%async_computation.33 | async-start | bytes 3244032 | tf_op jit(solution)/shard_map/reduce_scatter | solution.py:354
  2188.9 196.5 %reduce-scatter.39.cloned.1.call-start = ((), (), s32[]{:S(2)}) async-start(), calls=%async_computation.34 | async-start | bytes 3244032 | tf_op jit(solution)/shard_map/reduce_scatter | solution.py:355
  2196.8 237.3 %reduce-scatter.41.cloned.1.call-start = ((), (), s32[]{:S(2)}) async-start(), calls=%async_computation.35 | async-start | bytes 3244032 | tf_op jit(solution)/shard_map/reduce_scatter | solution.py:356
  2204.7 269.0 %reduce-scatter.27.cloned.1.call-start = ((), (), s32[]{:S(2)}) async-start(), calls=%async_computation.28 | async-start | bytes 1179648 | tf_op jit(solution)/shard_map/reduce_scatter | solution.py:347
  2209.7 303.7 %reduce-scatter.29.cloned.1.call-start = ((), (), s32[]{:S(2)}) async-start(), calls=%async_computation.29 | async-start | bytes 1179648 | tf_op jit(solution)/shard_map/reduce_scatter | solution.py:348
  2214.3 344.2 %reduce-scatter.35.cloned.1.call-start = ((), (), s32[]{:S(2)}) async-start(), calls=%async_computation.32 | async-start | bytes 2359296 | tf_op jit(solution)/shard_map/reduce_scatter | solution.py:353
  2220.9 382.6 %reduce-scatter.31.cloned.1.call-start = ((), (), s32[]{:S(2)}) async-start(), calls=%async_computation.30 | async-start | bytes 2359296 | tf_op jit(solution)/shard_map/reduce_scatter | solution.py:349
  2227.5 420.9 %reduce-scatter.33.cloned.1.call-start = ((), (), s32[]{:S(2)}) async-start(), calls=%async_computation.31 | async-start | bytes 2359296 | tf_op jit(solution)/shard_map/reduce_scatter | solution.py:350
  2233.4 549.4 %all-reduce.32.cloned.1.call-start = ((), (), s32[]{:S(2)}) async-start(), calls=%async_computation.38 | async-start | bytes 151552 | tf_op jit(solution)/shard_map/psum | solution.py:312
  (97 other events, 2905.7 us)
Sparse Core Ops, SparseCore 0:
  11.5 79.2 all-gather.10
  92.7 24.5 all-gather.12
  144.3 23.4 all-gather.16
  687.2 145.5 reduce-scatter.18
  834.5 26.2 all-gather.20
  862.9 78.0 all-gather.18
  942.9 26.3 all-gather.22
  971.2 25.1 all-gather.24
  997.9 78.0 all-gather.26
  1097.5 145.3 reduce-scatter.22
  1245.1 77.8 reduce-scatter.20
  1327.8 78.5 all-gather.28
  2136.4 35.2 reduce-scatter.42
  2174.6 34.1 reduce-scatter.44
  2211.0 76.7 reduce-scatter.24
  2291.6 45.2 reduce-scatter.36
  2340.7 44.6 reduce-scatter.38
  2389.4 44.6 reduce-scatter.40
  2437.7 35.9 reduce-scatter.26
  2477.5 35.9 reduce-scatter.28
  2517.3 41.1 reduce-scatter.34
  2562.3 41.1 reduce-scatter.30
  2607.2 41.0 reduce-scatter.32
  2656.5 126.3 all-reduce.31
  (1 shorter events, 23.3 us)
where the time goes:
time: 2810 us; the launch traced here: 2800 us
  waiting for transfers between devices  1240 us (44%)
  other arithmetic  813 us (29%)
  matrix products  506 us (18%)
  local copies, waits for them, and re-layouts  182 us (6%)
  blocking collectives  36.2 us (1%)
    another operation x64, other arithmetic, advance(): lax.linalg.triangular_solve(system, source, left_side=True, lower=True)  632 us
    reduce_scatter x1, waiting for transfers between devices, shards(): lax.psum_scatter(jnp.dot(mixed, full_output, preferred_element_type=jnp.f...  145 us
    reduce_scatter x1, waiting for transfers between devices, shards(): lax.psum_scatter(times_transposed(gate_grad, back_gate) + times_transpose...  137 us
    psum x1, waiting for transfers between devices, shards(): lax.psum((grad_norm_one, grad_norm_two, pulled[11], placed_query, placed_...  135 us
    all_gather x1, waiting for transfers between devices, shards(): rows_two = lax.all_gather(normed_two, 'tensor', axis=0, tiled=True)  80.2 us
    all_gather x1, waiting for transfers between devices, shards(): lax.all_gather(residual_grad.astype(jnp.bfloat16), 'tensor', axis=0, tile...  79.5 us
    all_gather x1, waiting for transfers between devices, shards(): lax.all_gather(middle_grad.astype(jnp.bfloat16), 'tensor', axis=0, tiled=...  78.7 us
    reduce_scatter x1, waiting for transfers between devices, shards(): lax.psum_scatter(jnp.dot(hidden, full_down, preferred_element_type=jnp.fl...  77.2 us
  transfers between devices with their start and end apart: 25, of which 20 were waited for; matrix products, arithmetic and copies ran while one was open for 26% of the time, Pallas kernels for 0%

commit v1 on v0

--- a/solution.py
+++ b/solution.py
@@ -1,114 +1,398 @@
+import functools
 import jax
 import jax.numpy as jnp
 from jax import lax
+from jax.experimental import pallas as pl
+from jax.experimental.pallas import tpu as pltpu
 from jax.sharding import PartitionSpec as P
 
 DK = 128
 DV = 256
-SPAN = 64
 SLOT = 1024
-
-
-def causal_filter(inputs, taps):
-    length = inputs.shape[1]
-    width = taps.shape[0]
-    padded = jnp.pad(inputs, ((0, 0), (width - 1, 0), (0, 0)))
-    total = jnp.zeros_like(inputs)
-    for offset in range(width):
-        total = total + taps[offset] * padded[:, offset : offset + length]
-    return jax.nn.silu(total)
-
-
-def unit_rows(values):
-    return values * lax.rsqrt(jnp.sum(values * values, -1, keepdims=True) + 1e-06)
-
-
-def span_rule(queries, keys, values, writes, decays):
-    rows, heads, length, kdim = queries.shape
-    vdim = values.shape[-1]
-    count = length // SPAN
-    highest = lax.Precision.HIGHEST
-
-    def blocks(array):
-        shaped = array.reshape((rows, heads, count, SPAN) + array.shape[3:])
-        return jnp.moveaxis(shaped, 2, 0)
-
-    strict = jnp.tril(jnp.ones((SPAN, SPAN), jnp.float32), -1)
-    causal = jnp.tril(jnp.ones((SPAN, SPAN), jnp.float32))
-    identity = jnp.eye(SPAN, dtype=jnp.float32)
-
-    def advance(state, block):
-        block_q, block_k, block_v, block_w, block_d = block
-        cumulative = jnp.cumsum(block_d, -1)
-        spread = jnp.exp(jnp.minimum(cumulative[..., :, None] - cumulative[..., None, :], 0.0))
-        keys_keys = jnp.einsum("rhid,rhjd->rhij", block_k, block_k, precision=highest)
-        system = identity + block_w[..., :, None] * spread * keys_keys * strict
-        growth = jnp.exp(cumulative)
-        source = block_w[..., None] * block_v - (block_w * growth)[..., None] * jnp.einsum(
-            "rhid,rhde->rhie", block_k, state, precision=highest
+LANES = 128
+BLOCK = 256
+F32 = jnp.float32
+BF16 = jnp.bfloat16
+
+
+def dot(left, right, dim_left, dim_right):
+    return lax.dot_general(
+        left, right, (((dim_left,), (dim_right,)), ((), ())), preferred_element_type=F32
+    )
+
+
+def halves(value):
+    high = value.astype(BF16)
+    return high, (value - high.astype(F32)).astype(BF16)
+
+
+def mm(left, right, dim_left=1, dim_right=0):
+    left_high, left_low = halves(left)
+    right_high, right_low = halves(right)
+    return (
+        dot(left_high, right_high, dim_left, dim_right)
+        + dot(left_high, right_low, dim_left, dim_right)
+        + dot(left_low, right_high, dim_left, dim_right)
+    )
+
+
+def mm_full(left, right, dim_left, dim_right):
+    return lax.dot_general(
+        left,
+        right,
+        (((dim_left,), (dim_right,)), ((), ())),
+        preferred_element_type=F32,
+        precision=lax.Precision.HIGHEST,
+    )
+
+
+def sigmoid(value):
+    return 1.0 / (1.0 + jnp.exp(-value))
+
+
+def softplus(value):
+    return jnp.maximum(value, 0.0) + jnp.log1p(jnp.exp(-jnp.abs(value)))
+
+
+def valid_rows(first, count, start, end):
+    position = first + lax.broadcasted_iota(jnp.int32, (count, 1), 0)
+    return jnp.where((position >= start) & (position < end), 1.0, 0.0).astype(F32)
+
+
+def convolve(extended, taps, count):
+    total = taps[0:1, :] * extended[5 : 5 + count]
+    for offset in range(1, 4):
+        total = total + taps[offset : offset + 1, :] * extended[5 + offset : 5 + offset + count]
+    return total
+
+
+def unit_scale(value):
+    return lax.rsqrt(jnp.sum(value * value, -1, keepdims=True) + 1e-06)
+
+
+def triangle(size):
+    row = lax.broadcasted_iota(jnp.int32, (size, size), 0)
+    column = lax.broadcasted_iota(jnp.int32, (size, size), 1)
+    return row, column
+
+
+def lower_ones(size):
+    row, column = triangle(size)
+    return jnp.where(row >= column, 1.0, 0.0).astype(F32)
+
+
+def inverses(systems, size):
+    row, column = triangle(size)
+    differ = jnp.bitwise_xor(row, column)
+    eye = jnp.where(differ == 0, 1.0, 0.0).astype(F32)
+    found = [eye - jnp.where(differ == 1, system, 0.0) for system in systems]
+    width = 2
+    while width < size:
+        mask = (differ >= width) & (differ < 2 * width)
+        parts = [jnp.where(mask, system, 0.0) for system in systems]
+        middle = [mm(f, p) for f, p in zip(found, parts)]
+        found = [f - mm(m, f) for f, m in zip(found, middle)]
+        width *= 2
+    return found
+
+
+def gather_inputs(first, start, end, refs, heads, block):
+    pre_q, pre_k, pre_v, pre_ab, halo_q, halo_k, halo_v, taps_q, taps_k, taps_v, rate, bias = refs
+    valid = valid_rows(first, block, start, end)
+    halo_valid = valid_rows(first - 8, 8, start, end)
+    ext_q = jnp.concatenate([halo_q[...] * halo_valid, pre_q[...] * valid], 0)
+    ext_k = jnp.concatenate([halo_k[...] * halo_valid, pre_k[...] * valid], 0)
+    ext_v = jnp.concatenate([halo_v[...] * halo_valid, pre_v[...] * valid], 0)
+    conv_q = convolve(ext_q, taps_q[...], block)
+    conv_k = convolve(ext_k, taps_k[...], block)
+    conv_v = convolve(ext_v, taps_v[...], block)
+    both = pre_ab[...]
+    shifted = both + bias[...]
+    decay = rate[...] * softplus(shifted) * valid
+    strength = sigmoid(both) * valid
+    ones = lower_ones(block)
+    cum = mm_full(ones, decay, 1, 0)
+    cum_rows = mm_full(decay, ones, 0, 1)
+    return dict(
+        valid=valid, ext=(ext_q, ext_k, ext_v), conv=(conv_q, conv_k, conv_v), shifted=shifted,
+        decay=decay, strength=strength, ones=ones, cum=cum, cum_rows=cum_rows,
+    )
+
+
+def head_operands(common, head, heads, block):
+    conv_q, conv_k, conv_v = common["conv"]
+    keys = slice(head * DK, (head + 1) * DK)
+    vals = slice(head * DV, (head + 1) * DV)
+    u_q, u_k, u_v = conv_q[:, keys], conv_k[:, keys], conv_v[:, vals]
+    s_q, s_k, s_v = sigmoid(u_q), sigmoid(u_k), sigmoid(u_v)
+    y_q, y_k = u_q * s_q, u_k * s_k
+    n_q, n_k = unit_scale(y_q), unit_scale(y_k)
+    cum = common["cum"][:, head : head + 1]
+    cum_row = common["cum_rows"][head : head + 1, :]
+    last = common["cum"][block - 1 : block, head : head + 1]
+    spread = jnp.exp(jnp.minimum(cum - cum_row, 0.0))
+    return dict(
+        u=(u_q, u_k, u_v), s=(s_q, s_k, s_v), n=(n_q, n_k), unit=(y_q * n_q, y_k * n_k),
+        q=y_q * (n_q * DK ** (-0.5)), k=y_k * (n_k * common["valid"]), v=u_v * s_v,
+        beta=common["strength"][:, heads + head : heads + head + 1],
+        growth=jnp.exp(cum), remain=jnp.exp(last - cum), whole=jnp.exp(last), spread=spread,
+    )
+
+
+def forward_kernel(heads, block, bounds, pre_q, pre_k, pre_v, pre_g, pre_ab, halo_q, halo_k, halo_v,
+                   taps_q, taps_k, taps_v, rate, bias, gain, mixed, out, states, deltas, solves, state):
+    row, step = pl.program_id(0), pl.program_id(1)
+
+    @pl.when(step == 0)
+    def _():
+        state[...] = jnp.zeros_like(state)
+
+    refs = (pre_q, pre_k, pre_v, pre_ab, halo_q, halo_k, halo_v, taps_q, taps_k, taps_v, rate, bias)
+    common = gather_inputs(step * block, bounds[0, row], bounds[1, row], refs, heads, block)
+    ops = [head_operands(common, head, heads, block) for head in range(heads)]
+    at, to = triangle(block)
+    systems = [jnp.where(at > to, o["beta"] * o["spread"] * mm(o["k"], o["k"], 1, 1), 0.0) for o in ops]
+    found = inverses(systems, block)
+    for head, o in enumerate(ops):
+        vals = slice(head * DV, (head + 1) * DV)
+        old = state[head]
+        states[head] = old.astype(states.dtype)
+        source = o["beta"] * o["v"] - (o["beta"] * o["growth"]) * mm(o["k"], old)
+        delta = mm(found[head], source)
+        scores = jnp.where(at >= to, o["spread"] * mm(o["q"], o["k"], 1, 1), 0.0)
+        emitted = o["growth"] * mm(o["q"], old) + mm(scores, delta)
+        state[head] = o["whole"] * old + mm(o["k"] * o["remain"], delta, 0, 0)
+        solves[head] = found[head].astype(solves.dtype)
+        deltas[:, vals] = delta.astype(deltas.dtype)
+        out[:, vals] = emitted.astype(out.dtype)
+        scale = lax.rsqrt(jnp.mean(emitted * emitted, -1, keepdims=True) + 1e-05)
+        gate = pre_g[:, vals]
+        mixed[:, vals] = (
+            emitted * scale * gain[...] * (gate * sigmoid(gate)) * common["valid"]
+        ).astype(mixed.dtype)
+
+
+def backward_kernel(heads, block, steps, bounds, pre_q, pre_k, pre_v, pre_g, pre_ab, halo_q, halo_k, halo_v,
+                    taps_q, taps_k, taps_v, rate, bias, gain, out, states, deltas, solves, grad,
+                    d_q, d_k, d_v, d_g, d_ab, d_taps_q, d_taps_k, d_taps_v, d_small, d_gain,
+                    d_state, next_q, next_k, next_v):
+    row, back = pl.program_id(0), pl.program_id(1)
+    step = steps - 1 - back
+
+    @pl.when((row == 0) & (back == 0))
+    def _():
+        for ref in (d_taps_q, d_taps_k, d_taps_v, d_small, d_gain):
+            ref[...] = jnp.zeros_like(ref)
+
+    @pl.when(back == 0)
+    def _():
+        for ref in (d_state, next_q, next_k, next_v):
+            ref[...] = jnp.zeros_like(ref)
+
+    refs = (pre_q, pre_k, pre_v, pre_ab, halo_q, halo_k, halo_v, taps_q, taps_k, taps_v, rate, bias)
+    common = gather_inputs(step * block, bounds[0, row], bounds[1, row], refs, heads, block)
+    valid = common["valid"]
+    at, to = triangle(block)
+    lane = lax.broadcasted_iota(jnp.int32, (block, LANES), 1)
+    ones_cols = jnp.ones((block, LANES), BF16)
+    d_cum = jnp.zeros((block, LANES), F32)
+    d_last = jnp.zeros((1, LANES), F32)
+    d_beta = jnp.zeros((block, LANES), F32)
+    du_q, du_k, du_v = [], [], []
+    gain_sum = jnp.zeros((1, DV), F32)
+    for head in range(heads):
+        o = head_operands(common, head, heads, block)
+        vals = slice(head * DV, (head + 1) * DV)
+        q, k, v, beta, growth, remain, whole, spread = (
+            o[name] for name in ("q", "k", "v", "beta", "growth", "remain", "whole", "spread"))
+        emitted = out[:, vals].astype(F32)
+        scale = lax.rsqrt(jnp.mean(emitted * emitted, -1, keepdims=True) + 1e-05)
+        unit = emitted * scale
+        gate = pre_g[:, vals]
+        s_g = sigmoid(gate)
+        d_mixed = grad[:, vals].astype(F32) * valid
+        d_g[:, vals] = (d_mixed * unit * gain[...] * (s_g * (1.0 + gate * (1.0 - s_g)))).astype(d_g.dtype)
+        part = d_mixed * (gate * s_g)
+        gain_sum = gain_sum + jnp.sum(part * unit, 0, keepdims=True)
+        weighted = part * gain[...]
+        d_out = scale * (weighted - unit * jnp.mean(weighted * unit, -1, keepdims=True))
+        old = states[head].astype(F32)
+        delta = deltas[:, vals]
+        solve = solves[head]
+        d_new = d_state[head]
+        q_k = mm(q, k, 1, 1)
+        k_k = mm(k, k, 1, 1)
+        scores = jnp.where(at >= to, spread * q_k, 0.0)
+        linked = jnp.where(at > to, spread * k_k, 0.0)
+        k_s = mm(k, old)
+        q_s = mm(q, old)
+        k_rem = k * remain
+        d_delta = mm(scores, d_out, 0, 0) + mm(k_rem, d_new)
+        d_source = mm(solve, d_delta, 0, 0)
+        d_system = -mm(d_source, delta, 1, 1)
+        d_scores = mm(d_out, delta, 1, 1)
+        d_qk = jnp.where(at >= to, d_scores * spread, 0.0)
+        by_link = d_system * linked
+        d_kk = jnp.where(at > to, beta * d_system * spread, 0.0)
+        edge, edge_low = halves(d_scores * scores + beta * by_link)
+        d_query = growth * mm(d_out, old, 1, 1) + mm(d_qk, k)
+        back_state = mm(delta, d_new, 1, 1)
+        d_key = (
+            mm((beta * growth) * d_source, old, 1, 1) * (-1.0)
+            + mm(d_qk, q, 0, 0)
+            + mm(d_kk, k)
+            + mm(d_kk, k, 0, 0)
+            + remain * back_state
         )
-        delta = lax.linalg.triangular_solve(system, source, left_side=True, lower=True)
-        scores = (
-            jnp.einsum("rhid,rhjd->rhij", block_q, block_k, precision=highest) * spread * causal
+        d_value = beta * d_source
+        lose = jnp.sum(k_rem * back_state, -1, keepdims=True)
+        pull = jnp.sum(d_source * k_s, -1, keepdims=True)
+        grow = growth * (jnp.sum(d_out * q_s, -1, keepdims=True) - beta * pull)
+        d_b = jnp.sum(d_source * v, -1, keepdims=True) - growth * pull + jnp.sum(by_link, -1, keepdims=True)
+        cut = (
+            dot(edge, ones_cols, 1, 0) - dot(edge, ones_cols, 0, 0)
+            + dot(edge_low, ones_cols, 1, 0) - dot(edge_low, ones_cols, 0, 0)
         )
-        emitted = growth[..., None] * jnp.einsum(
-            "rhid,rhde->rhie", block_q, state, precision=highest
+        d_cum = jnp.where(lane == head, cut + (grow - lose), d_cum)
+        d_beta = jnp.where(lane == heads + head, d_b, d_beta)
+        total = jnp.sum(lose, keepdims=True) + whole * jnp.sum(old * d_new, keepdims=True)
+        d_last = jnp.where(lane[0:1] == head, total, d_last)
+        d_state[head] = (
+            whole * d_new + mm(q, growth * d_out, 0, 0) - mm(k * (beta * growth), d_source, 0, 0)
         )
-        emitted = emitted + jnp.einsum("rhij,rhje->rhie", scores, delta, precision=highest)
-        remain = jnp.exp(cumulative[..., -1:] - cumulative)
-        new_state = jnp.exp(cumulative[..., -1])[..., None, None] * state
-        new_state = new_state + jnp.einsum(
-            "rhid,rhie->rhde", block_k * remain[..., None], delta, precision=highest
-        )
-        return (new_state, emitted)
-
-    start_state = jnp.zeros((rows, heads, kdim, vdim), jnp.float32)
-    _, outputs = lax.scan(
-        jax.checkpoint(advance),
-        start_state,
-        (blocks(queries), blocks(keys), blocks(values), blocks(writes), blocks(decays)),
-    )
-    return jnp.moveaxis(outputs, 0, 2).reshape(rows, heads, length, vdim)
-
-
-def mixing(
-    proj_query,
-    proj_key,
-    proj_value,
-    proj_gate,
-    proj_decay,
-    proj_strength,
-    filter_query,
-    filter_key,
-    filter_value,
-    decay_log,
-    decay_bias,
-    head_gain,
-    row_mask,
-):
-    rows, length = row_mask.shape
-    heads = proj_decay.shape[-1]
-    valid = row_mask[..., None]
-    queries = causal_filter(proj_query * valid, filter_query).reshape(rows, length, heads, DK)
-    keys = causal_filter(proj_key * valid, filter_key).reshape(rows, length, heads, DK)
-    values = causal_filter(proj_value * valid, filter_value).reshape(rows, length, heads, DV)
-    queries = unit_rows(queries) * DK ** (-0.5)
-    keys = unit_rows(keys) * valid[..., None]
-    writes = jax.nn.sigmoid(proj_strength) * valid
-    decays = -jnp.exp(decay_log) * jax.nn.softplus(proj_decay + decay_bias) * valid
-    outputs = span_rule(
-        jnp.moveaxis(queries, 2, 1),
-        jnp.moveaxis(keys, 2, 1),
-        jnp.moveaxis(values, 2, 1),
-        jnp.moveaxis(writes, 2, 1),
-        jnp.moveaxis(decays, 2, 1),
-    )
-    outputs = jnp.moveaxis(outputs, 1, 2)
-    outputs = (
-        outputs * lax.rsqrt(jnp.mean(outputs * outputs, -1, keepdims=True) + 1e-05) * head_gain
-    )
-    gating = jax.nn.silu(proj_gate).reshape(rows, length, heads, DV)
-    return (outputs * gating * valid[..., None]).reshape(rows, length, heads * DV)
+        unit_q, unit_k = o["unit"]
+        n_q, n_k = o["n"]
+        d_unit = d_query * DK ** (-0.5)
+        d_yq = n_q * (d_unit - unit_q * jnp.sum(unit_q * d_unit, -1, keepdims=True))
+        d_unit = d_key * valid
+        d_yk = n_k * (d_unit - unit_k * jnp.sum(unit_k * d_unit, -1, keepdims=True))
+        for store, d_y, u, s in zip((du_q, du_k, du_v), (d_yq, d_yk, d_value), o["u"], o["s"]):
+            store.append(d_y * (s * (1.0 + u * (1.0 - s))))
+    d_decay = mm_full(common["ones"], d_cum, 0, 0) + d_last
+    slope = d_decay * rate[...] * sigmoid(common["shifted"]) * valid
+    strength = common["strength"]
+    d_pre_b = d_beta * strength * (1.0 - strength)
+    d_ab[...] = (slope + d_pre_b).astype(d_ab.dtype)
+    d_small[0:1, :] += jnp.sum(d_decay * common["decay"], 0, keepdims=True)
+    d_small[1:2, :] += jnp.sum(slope, 0, keepdims=True)
+    d_gain[0:1, :] += gain_sum
+    for store, ext, taps, d_taps, later, target in zip(
+        (du_q, du_k, du_v), common["ext"], (taps_q, taps_k, taps_v), (d_taps_q, d_taps_k, d_taps_v),
+        (next_q, next_k, next_v), (d_q, d_k, d_v),
+    ):
+        du = jnp.concatenate(store, 1) if heads > 1 else store[0]
+        longer = jnp.concatenate([du, later[...]], 0)
+        later[...] = du[0:8]
+        total = taps[3:4, :] * du
+        for offset in range(3):
+            total = total + taps[offset : offset + 1, :] * longer[3 - offset : 3 - offset + block]
+        target[...] = (total * valid).astype(target.dtype)
+        for offset in range(4):
+            d_taps[offset : offset + 1, :] += jnp.sum(du * ext[5 + offset : 5 + offset + block], 0, keepdims=True)
+
+
+def input_specs(heads, block, place):
+    wide_k, wide_v = heads * DK, heads * DV
+
+    def tile(width):
+        return pl.BlockSpec((None, block, width), lambda r, c, *_: (r, place(c), 0))
+
+    def halo(width):
+        return pl.BlockSpec(
+            (None, 8, width), lambda r, c, *_: (r, jnp.maximum(place(c) * (block // 8) - 1, 0), 0))
+
+    def fixed(rows, width):
+        return pl.BlockSpec((rows, width), lambda r, c, *_: (0, 0))
+
+    return [
+        tile(wide_k), tile(wide_k), tile(wide_v), tile(wide_v), tile(LANES),
+        halo(wide_k), halo(wide_k), halo(wide_v),
+        fixed(8, wide_k), fixed(8, wide_k), fixed(8, wide_v),
+        fixed(1, LANES), fixed(1, LANES), fixed(1, DV),
+    ]
+
+
+def operands(pre_q, pre_k, pre_v, pre_g, pre_ab, taps_q, taps_k, taps_v, rate, bias, gain):
+    return (pre_q, pre_k, pre_v, pre_g, pre_ab, pre_q, pre_k, pre_v, taps_q, taps_k, taps_v, rate, bias, gain)
+
+
+def mixer_forward(bounds, heads, block, *values):
+    rows = values[0].shape[0]
+    steps = SLOT // block
+    wide_v = heads * DV
+    tile_v = pl.BlockSpec((None, block, wide_v), lambda r, c, *_: (r, c, 0))
+    return pl.pallas_call(
+        functools.partial(forward_kernel, heads, block),
+        grid_spec=pltpu.PrefetchScalarGridSpec(
+            num_scalar_prefetch=1,
+            grid=(rows, steps),
+            in_specs=input_specs(heads, block, lambda c: c),
+            out_specs=[
+                tile_v, tile_v,
+                pl.BlockSpec((None, None, heads, DK, DV), lambda r, c, *_: (r, c, 0, 0, 0)),
+                tile_v,
+                pl.BlockSpec((None, None, heads, block, block), lambda r, c, *_: (r, c, 0, 0, 0)),
+            ],
+            scratch_shapes=[pltpu.VMEM((heads, DK, DV), F32)],
+        ),
+        out_shape=[
+            jax.ShapeDtypeStruct((rows, SLOT, wide_v), BF16),
+            jax.ShapeDtypeStruct((rows, SLOT, wide_v), F32),
+            jax.ShapeDtypeStruct((rows, steps, heads, DK, DV), F32),
+            jax.ShapeDtypeStruct((rows, SLOT, wide_v), F32),
+            jax.ShapeDtypeStruct((rows, steps, heads, block, block), F32),
+        ],
+        name="mixer_forward",
+    )(bounds, *operands(*values))
+
+
+def mixer_backward(bounds, heads, block, values, saved, grad):
+    rows = values[0].shape[0]
+    steps = SLOT // block
+    wide_k, wide_v = heads * DK, heads * DV
+
+    def tile(width):
+        return pl.BlockSpec((None, block, width), lambda r, c, *_: (r, steps - 1 - c, 0))
+
+    def fixed(rows, width):
+        return pl.BlockSpec((rows, width), lambda r, c, *_: (0, 0))
+
+    out, states, deltas, solves = saved
+    return pl.pallas_call(
+        functools.partial(backward_kernel, heads, block, steps),
+        grid_spec=pltpu.PrefetchScalarGridSpec(
+            num_scalar_prefetch=1,
+            grid=(rows, steps),
+            in_specs=input_specs(heads, block, lambda c: steps - 1 - c) + [
+                tile(wide_v),
+                pl.BlockSpec((None, None, heads, DK, DV), lambda r, c, *_: (r, steps - 1 - c, 0, 0, 0)),
+                tile(wide_v),
+                pl.BlockSpec((None, None, heads, block, block), lambda r, c, *_: (r, steps - 1 - c, 0, 0, 0)),
+                tile(wide_v),
+            ],
+            out_specs=[
+                tile(wide_k), tile(wide_k), tile(wide_v), tile(wide_v), tile(LANES),
+                fixed(8, wide_k), fixed(8, wide_k), fixed(8, wide_v), fixed(8, LANES), fixed(8, DV),
+            ],
+            scratch_shapes=[
+                pltpu.VMEM((heads, DK, DV), F32),
+                pltpu.VMEM((8, wide_k), F32), pltpu.VMEM((8, wide_k), F32), pltpu.VMEM((8, wide_v), F32),
+            ],
+        ),
+        out_shape=[
+            jax.ShapeDtypeStruct((rows, SLOT, wide_k), BF16),
+            jax.ShapeDtypeStruct((rows, SLOT, wide_k), BF16),
+            jax.ShapeDtypeStruct((rows, SLOT, wide_v), BF16),
+            jax.ShapeDtypeStruct((rows, SLOT, wide_v), BF16),
+            jax.ShapeDtypeStruct((rows, SLOT, LANES), BF16),
+            jax.ShapeDtypeStruct((8, wide_k), F32),
+            jax.ShapeDtypeStruct((8, wide_k), F32),
+            jax.ShapeDtypeStruct((8, wide_v), F32),
+            jax.ShapeDtypeStruct((8, LANES), F32),
+            jax.ShapeDtypeStruct((8, DV), F32),
+        ],
+        name="mixer_backward",
+    )(bounds, *operands(*values), out, states, deltas, solves, grad)
 
 
 def inner_rows(left, right):
@@ -209,10 +493,15 @@
         head_gain,
     )
 
-    def local_mixing(*values):
-        return mixing(*values, row_mask)
-
-    mixed_float, pull_mixing = jax.vjp(local_mixing, *projections + local_params)
+    local_q, local_k, local_v, local_log, local_bias, _ = local_params
+    pad = LANES - 2 * heads_local
+    both = jnp.pad(jnp.concatenate(projections[4:6], -1), ((0, 0), (0, 0), (0, pad)))
+    rate = jnp.pad(-jnp.exp(local_log), (0, LANES - heads_local))[None]
+    bias = jnp.pad(local_bias, (0, LANES - heads_local))[None]
+    taps = tuple(jnp.pad(t, ((0, 4), (0, 0))) for t in (local_q, local_k, local_v))
+    bounds = jnp.stack([starts, starts + lengths])
+    values = projections[:4] + (both,) + taps + (rate, bias, head_gain[None])
+    mixed_float, *saved = mixer_forward(bounds, heads_local, BLOCK, *values)
     mixed = mixed_float.reshape(rows * SLOT, -1).astype(jnp.bfloat16)
     attention = lax.psum_scatter(
         jnp.dot(mixed, full_output, preferred_element_type=jnp.float32),
@@ -280,7 +569,13 @@
     attention_grad = lax.all_gather(middle_grad.astype(jnp.bfloat16), "tensor", axis=0, tiled=True)
     mixed_grad = times_transposed(attention_grad, back_output)
     grad_output = inner_rows(mixed, attention_grad)
-    pulled = pull_mixing(mixed_grad.reshape(rows, SLOT, -1))
+    g = mixer_backward(
+        bounds, heads_local, BLOCK, values, saved, mixed_grad.reshape(rows, SLOT, -1)
+    )
+    both_grad = g[4][..., :heads_local], g[4][..., heads_local : 2 * heads_local]
+    pulled = tuple(g[:4]) + both_grad + (
+        g[5][:4], g[6][:4], g[7][:4], g[8][0, :heads_local], g[8][1, :heads_local], g[9][0]
+    )
     projection_grads = tuple(
         (grad.reshape(rows * SLOT, -1).astype(jnp.bfloat16) for grad in pulled[:6])
     )

time: 2810 us -> 1690 us (0.60)
  other arithmetic: 813 us -> 23.7 us
  matrix products: 506 us -> 183 us
  local copies, waits for them, and re-layouts: 182 us -> 20.8 us
  Pallas kernels: 0 us -> 128 us
  waiting for transfers between devices: 1240 us -> 1270 us
    another operation x144 -> x1, other arithmetic: 664 us -> 0.57 us  [shards(): bounds = jnp.stack([starts, starts + lengths])]
    dot_general x368 -> x0, matrix products: 289 us -> none  [the longest x64 64.1 us: advance(): jnp.einsum('rhid,rhde->rhie', block_k, state, precision=highest)]
    pallas_call x0 -> x2, Pallas kernels: none -> 128 us  [the longest x1 67.2 us: mixer_backward(): pl.pallas_call(functools.partial(backward_kernel, heads, block, steps), g...]
    squeeze x96 -> x0, local copies, waits for them, and re-layouts: 75.4 us -> none  [span_rule(): lax.scan(jax.checkpoint(advance), start_state, (blocks(queries), blocks(k...]
    reduce_sum x57 -> x0, other arithmetic: 37.8 us -> none  [the longest x2 9.68 us: causal_filter(): total = total + taps[offset] * padded[:, offset:offset + length]]
    mul x88 -> x0, other arithmetic: 35.1 us -> none  [the longest x32 12.2 us: advance(): block_w * growth]
  transfers between devices with their start and end apart: 25 -> 25, of which waited for: 20 -> 22; matrix products, arithmetic and copies ran while one was open for 26% -> 10% of each run, Pallas kernels for 0% -> 4%
where the time goes in v1:
time: 1690 us; the launch traced here: 1680 us
  waiting for transfers between devices  1270 us (75%)
  matrix products  183 us (11%)
  Pallas kernels  128 us (8%)
  blocking collectives  36.2 us (2%)
  other arithmetic  23.7 us (1%)
  local copies, waits for them, and re-layouts  20.8 us (1%)
    reduce_scatter x1, waiting for transfers between devices, shards(): lax.psum_scatter(jnp.dot(mixed, full_output, preferred_element_type=jnp.f...  144 us
    reduce_scatter x1, waiting for transfers between devices, shards(): lax.psum_scatter(times_transposed(gate_grad, back_gate) + times_transpose...  137 us
    psum x1, waiting for transfers between devices, shards(): lax.psum((grad_norm_one, grad_norm_two, pulled[11], placed_query, placed_...  134 us
    all_gather x1, waiting for transfers between devices, shards(): rows_two = lax.all_gather(normed_two, 'tensor', axis=0, tiled=True)  80.2 us
    all_gather x1, waiting for transfers between devices, shards(): lax.all_gather(residual_grad.astype(jnp.bfloat16), 'tensor', axis=0, tile...  79.5 us
    all_gather x1, waiting for transfers between devices, shards(): lax.all_gather(middle_grad.astype(jnp.bfloat16), 'tensor', axis=0, tiled=...  78.7 us
    reduce_scatter x1, waiting for transfers between devices, shards(): lax.psum_scatter(jnp.dot(hidden, full_down, preferred_element_type=jnp.fl...  77.2 us
    dot_general x10, matrix products, times_transposed(): lax.dot_general(left, right, (((1,), (1,)), ((), ())), preferred_element_...  71.5 us
  transfers between devices with their start and end apart: 25, of which 22 were waited for; matrix products, arithmetic and copies ran while one was open for 10% of the time, Pallas kernels for 4%

profile of v1, /device:TPU:8, one launch (start us, length us, event | category | flops | bytes accessed | tf_op | source)
XLA Modules:
  0.0 1681.0 jit_solution(14605150418946359664)
XLA Ops:
  53.6 37.2 %all-gather.11.cloned.1.call-done = bf16[2048,1024]{1,0:T(8,128)(2,1)} async-done(((bf16[512,1024]{1,0:T(8,128)(2,1)}), bf16[2048,1024]{1,0:T(8,128)(2,1)}) %all-gather.11.cloned.1.call-update) | async-done | bytes 4194320 | tf_op jit(solution)/shard_map/all_gather | solution.py:478
  124.0 18.5 %all-gather.13.cloned.1.call-done = bf16[1024,512]{1,0:T(8,128)(2,1)} async-done(((bf16[128,512]{1,0:T(8,128)(2,1)}), bf16[1024,512]{1,0:T(8,128)(2,1)}) %all-gather.13.cloned.1.call-update) | async-done | bytes 1048592 | tf_op jit(solution)/shard_map/all_gather | solution.py:454
  149.3 60.6 %mixer_forward.1 = (bf16[2,1024,512]{2,1,0:T(8,128)(2,1)}, f32[2,1024,512]{2,1,0:T(8,128)}, f32[2,4,2,128,256]{4,3,2,1,0:T(8,128)}, f32[2,1024,512]{2,1,0:T(8,128)}, f32[2,4,2,256,256]{4,3,2,1,0:T(8,128)}) custom-call(s32[2,2]{1,0:T(2,128)} %pad_add_fusion.bounds, f32[2,1024,256]{2,1,0:T(8,128)} %bitcast.101, f32[2,1024,256]{2,1,0:T(8,128)} %bitcast.97, ...), custom_call_target="tpu_custom_call" | custom-call | tf_op jit(solution)/shard_map/mixer_forward/pallas_call | solution.py:324
  218.1 143.7 %reduce-scatter.19.cloned.1.call-done = f32[512,1024]{1,0:T(8,128)} async-done(((f32[2048,1024]{1,0:T(8,128)}), f32[512,1024]{1,0:T(8,128)}) %reduce-scatter.19.cloned.1.call-update) | async-done | bytes 2097168 | tf_op jit(solution)/shard_map/reduce_scatter | solution.py:506
  368.0 21.8 %all-gather.23.cloned.1.call-done = bf16[1024,704]{0,1:T(8,128)(2,1)} async-done(((bf16[128,704]{0,1:T(8,128)(2,1)}), bf16[1024,704]{0,1:T(8,128)(2,1)}) %all-gather.23.cloned.1.call-update) | async-done | bytes 1441808 | tf_op jit(solution)/shard_map/all_gather | solution.py:460
  389.8 80.2 %all-gather.19.cloned.1.call-done = bf16[2048,1024]{1,0:T(8,128)(2,1)} async-done(((bf16[512,1024]{1,0:T(8,128)(2,1)}), bf16[2048,1024]{1,0:T(8,128)(2,1)}) %all-gather.19.cloned.1.call-update) | async-done | bytes 4194320 | tf_op jit(solution)/shard_map/all_gather | solution.py:515
  478.3 20.0 %all-gather.21.cloned.1.call-done = bf16[1024,704]{0,1:T(8,128)(2,1)} async-done(((bf16[128,704]{0,1:T(8,128)(2,1)}), bf16[1024,704]{0,1:T(8,128)(2,1)}) %all-gather.21.cloned.1.call-update) | async-done | bytes 1441808 | tf_op jit(solution)/shard_map/all_gather | solution.py:459
  506.6 18.8 %all-gather.25.cloned.1.call-done = bf16[704,1024]{1,0:T(8,128)(2,1)} async-done(((bf16[704,128]{1,0:T(8,128)(2,1)}), bf16[704,1024]{1,0:T(8,128)(2,1)}) %all-gather.25.cloned.1.call-update) | async-done | bytes 1441808 | tf_op jit(solution)/shard_map/all_gather | solution.py:461
  525.4 79.5 %all-gather.27.cloned.1.call-done = bf16[2048,1024]{1,0:T(8,128)(2,1)} async-done(((bf16[512,1024]{1,0:T(8,128)(2,1)}), bf16[2048,1024]{1,0:T(8,128)(2,1)}) %all-gather.27.cloned.1.call-update) | async-done | bytes 4194320 | tf_op jit(solution)/shard_map/all_gather | solution.py:551
  634.6 137.2 %reduce-scatter.23.cloned.1.call-done = f32[512,1024]{1,0:T(8,128)} async-done(((f32[2048,1024]{1,0:T(8,128)}), f32[512,1024]{1,0:T(8,128)}) %reduce-scatter.23.cloned.1.call-update) | async-done | bytes 2097168 | tf_op jit(solution)/shard_map/reduce_scatter | solution.py:561
  774.5 77.2 %reduce-scatter.21.cloned.1.call-done = bf16[512,1024]{1,0:T(8,128)(2,1)} async-done(((bf16[2048,1024]{1,0:T(8,128)(2,1)}), bf16[512,1024]{1,0:T(8,128)(2,1)}) %reduce-scatter.21.cloned.1.call-update) | async-done | bytes 1048592 | tf_op jit(solution)/shard_map/reduce_scatter | solution.py:519
  856.6 78.7 %all-gather.29.cloned.1.call-done = bf16[2048,1024]{1,0:T(8,128)(2,1)} async-done(((bf16[512,1024]{1,0:T(8,128)(2,1)}), bf16[2048,1024]{1,0:T(8,128)(2,1)}) %all-gather.29.cloned.1.call-update) | async-done | bytes 4194320 | tf_op jit(solution)/shard_map/all_gather | solution.py:569
  942.2 67.2 %mixer_backward.1 = (bf16[2,1024,256]{2,1,0:T(8,128)(2,1)}, bf16[2,1024,256]{2,1,0:T(8,128)(2,1)}, bf16[2,1024,512]{2,1,0:T(8,128)(2,1)}, bf16[2,1024,512]{2,1,0...) custom-call(s32[2,2]{1,0:T(2,128)} %pad_add_fusion.bounds, ...), custom_call_target="tpu_custom_call" | custom-call | tf_op jit(solution)/shard_map/mixer_backward/pallas_call | solution.py:361
  1042.4 16.3 add_convert_fusion
  1118.1 50.8 %reduce-scatter.25.cloned.1.call-done = bf16[512,1024]{1,0:T(8,128)(2,1)} async-done(((bf16[2048,1024]{1,0:T(8,128)(2,1)}), bf16[512,1024]{1,0:T(8,128)(2,1)}) %reduce-scatter.25.cloned.1.call-update) | async-done | bytes 1048592 | tf_op jit(solution)/shard_map/reduce_scatter | solution.py:587
  1174.7 43.2 %reduce-scatter.41.cloned.1.call-done = f32[704,128]{1,0:T(8,128)} async-done(((f32[704,1024]{1,0:T(8,128)}), f32[704,128]{1,0:T(8,128)}) %reduce-scatter.41.cloned.1.call-update) | async-done | bytes 360464 | tf_op jit(solution)/shard_map/reduce_scatter | solution.py:651
  1218.0 48.6 %reduce-scatter.37.cloned.1.call-done = f32[128,704]{0,1:T(8,128)} async-done(((f32[1024,704]{0,1:T(8,128)}), f32[128,704]{0,1:T(8,128)}) %reduce-scatter.37.cloned.1.call-update) | async-done | bytes 360464 | tf_op jit(solution)/shard_map/reduce_scatter | solution.py:649
  1266.5 48.7 %reduce-scatter.39.cloned.1.call-done = f32[128,704]{0,1:T(8,128)} async-done(((f32[1024,704]{0,1:T(8,128)}), f32[128,704]{0,1:T(8,128)}) %reduce-scatter.39.cloned.1.call-update) | async-done | bytes 360464 | tf_op jit(solution)/shard_map/reduce_scatter | solution.py:650
  1315.2 39.6 %reduce-scatter.29.cloned.1.call-done = f32[128,256]{1,0:T(8,128)} async-done(((f32[1024,256]{1,0:T(8,128)}), f32[128,256]{1,0:T(8,128)}) %reduce-scatter.29.cloned.1.call-update) | async-done | bytes 131088 | tf_op jit(solution)/shard_map/reduce_scatter | solution.py:643
  1354.8 39.7 %reduce-scatter.27.cloned.1.call-done = f32[128,256]{1,0:T(8,128)} async-done(((f32[1024,256]{1,0:T(8,128)}), f32[128,256]{1,0:T(8,128)}) %reduce-scatter.27.cloned.1.call-update) | async-done | bytes 131088 | tf_op jit(solution)/shard_map/reduce_scatter | solution.py:642
  1394.6 45.0 %reduce-scatter.35.cloned.1.call-done = f32[512,128]{1,0:T(8,128)} async-done(((f32[512,1024]{1,0:T(8,128)}), f32[512,128]{1,0:T(8,128)}) %reduce-scatter.35.cloned.1.call-update) | async-done | bytes 262160 | tf_op jit(solution)/shard_map/reduce_scatter | solution.py:648
  1439.6 45.0 %reduce-scatter.33.cloned.1.call-done = f32[128,512]{1,0:T(8,128)} async-done(((f32[1024,512]{1,0:T(8,128)}), f32[128,512]{1,0:T(8,128)}) %reduce-scatter.33.cloned.1.call-update) | async-done | bytes 262160 | tf_op jit(solution)/shard_map/reduce_scatter | solution.py:645
  1484.6 44.9 %reduce-scatter.31.cloned.1.call-done = f32[128,512]{1,0:T(8,128)} async-done(((f32[1024,512]{1,0:T(8,128)}), f32[128,512]{1,0:T(8,128)}) %reduce-scatter.31.cloned.1.call-update) | async-done | bytes 262160 | tf_op jit(solution)/shard_map/reduce_scatter | solution.py:644
  1529.4 134.5 %all-reduce.9.cloned.1.call-done = (f32[1024]{0:T(1024)}, f32[4,1024]{1,0:T(4,128)}, f32[4,1024]{1,0:T(4,128)}, f32[4,2048]{1,0:T(4,128)}, f32[8]{0:T(128)}, /*index=5*/f32[8]{0:T(128)}, f32[256]{0:T(256)}, f32[1024]{0:T(1024)}) async-done(((f32[1024]{0:T(1024)}, f32[4,1024]{1,0:T(4,128)}, f32[4,1024]{1,0:T(4,128)}, f32[4,2048]{1,0:T(4,128)}, f32[8]{0:T(128)}, /*index=5*/f32[8]{0:T(128)}, f32[256]{0:T(256)}, ...) | async-done | bytes 74832 | tf_op jit(solution)/shard_map/psum | solution.py:607
  (218 shorter events, 268.8 us)
Async XLA Ops:
  11.4 105.8 %all-gather.15.cloned.1.call-start = ((), (), s32[]{:S(2)}) async-start(), calls=%async_computation.16 | async-start | bytes 1179648 | tf_op jit(solution)/shard_map/all_gather | solution.py:455
  12.2 130.4 %all-gather.13.cloned.1.call-start = ((), (), s32[]{:S(2)}) async-start(), calls=%async_computation.15 | async-start | bytes 1179648 | tf_op jit(solution)/shard_map/all_gather | solution.py:454
  12.9 197.0 %all-gather.17.cloned.1.call-start = ((), (), s32[]{:S(2)}) async-start(), calls=%async_computation.17 | async-start | bytes 1179648 | tf_op jit(solution)/shard_map/all_gather | solution.py:458
  13.5 348.3 %reduce-scatter.19.cloned.1.call-start = ((), (), s32[]{:S(2)}) async-start(), calls=%async_computation.18 | async-start | bytes 10485760 | tf_op jit(solution)/shard_map/reduce_scatter | solution.py:506
  217.5 172.3 %all-gather.23.cloned.1.call-start = ((), (), s32[]{:S(2)}) async-start(), calls=%async_computation.21 | async-start | bytes 1622016 | tf_op jit(solution)/shard_map/all_gather | solution.py:460
  218.1 252.0 %all-gather.19.cloned.1.call-start = ((), (), s32[]{:S(2)}) async-start(), calls=%async_computation.19 | async-start | bytes 5242880 | tf_op jit(solution)/shard_map/all_gather | solution.py:515
  365.0 133.3 %all-gather.21.cloned.1.call-start = ((), (), s32[]{:S(2)}) async-start(), calls=%async_computation.20 | async-start | bytes 1622016 | tf_op jit(solution)/shard_map/all_gather | solution.py:459
  365.8 159.7 %all-gather.25.cloned.1.call-start = ((), (), s32[]{:S(2)}) async-start(), calls=%async_computation.22 | async-start | bytes 1622016 | tf_op jit(solution)/shard_map/all_gather | solution.py:461
  366.5 238.5 %all-gather.27.cloned.1.call-start = ((), (), s32[]{:S(2)}) async-start(), calls=%async_computation.24 | async-start | bytes 5242880 | tf_op jit(solution)/shard_map/all_gather | solution.py:551
  367.9 403.9 %reduce-scatter.23.cloned.1.call-start = ((), (), s32[]{:S(2)}) async-start(), calls=%async_computation.25 | async-start | bytes 10485760 | tf_op jit(solution)/shard_map/reduce_scatter | solution.py:561
  626.3 225.5 %reduce-scatter.21.cloned.1.call-start = ((), (), s32[]{:S(2)}) async-start(), calls=%async_computation.23 | async-start | bytes 5242880 | tf_op jit(solution)/shard_map/reduce_scatter | solution.py:519
  634.1 301.2 %all-gather.29.cloned.1.call-start = ((), (), s32[]{:S(2)}) async-start(), calls=%async_computation.26 | async-start | bytes 5242880 | tf_op jit(solution)/shard_map/all_gather | solution.py:569
  856.6 258.6 %reduce-scatter.43.cloned.1.call-start = ((), (), s32[]{:S(2)}) async-start(), calls=%async_computation.36 | async-start | bytes 589824
  1017.5 99.2 %reduce-scatter.45.cloned.1.call-start = ((), (), s32[]{:S(2)}) async-start(), calls=%async_computation.37 | async-start | bytes 589824
  1029.0 139.9 %reduce-scatter.25.cloned.1.call-start = ((), (), s32[]{:S(2)}) async-start(), calls=%async_computation.27 | async-start | bytes 5242880 | tf_op jit(solution)/shard_map/reduce_scatter | solution.py:587
  1058.8 159.2 %reduce-scatter.41.cloned.1.call-start = ((), (), s32[]{:S(2)}) async-start(), calls=%async_computation.35 | async-start | bytes 3244032 | tf_op jit(solution)/shard_map/reduce_scatter | solution.py:651
  1066.7 199.9 %reduce-scatter.37.cloned.1.call-start = ((), (), s32[]{:S(2)}) async-start(), calls=%async_computation.33 | async-start | bytes 3244032 | tf_op jit(solution)/shard_map/reduce_scatter | solution.py:649
  1074.8 240.4 %reduce-scatter.39.cloned.1.call-start = ((), (), s32[]{:S(2)}) async-start(), calls=%async_computation.34 | async-start | bytes 3244032 | tf_op jit(solution)/shard_map/reduce_scatter | solution.py:650
  1082.8 272.0 %reduce-scatter.29.cloned.1.call-start = ((), (), s32[]{:S(2)}) async-start(), calls=%async_computation.29 | async-start | bytes 1179648 | tf_op jit(solution)/shard_map/reduce_scatter | solution.py:643
  1087.6 307.0 %reduce-scatter.27.cloned.1.call-start = ((), (), s32[]{:S(2)}) async-start(), calls=%async_computation.28 | async-start | bytes 1179648 | tf_op jit(solution)/shard_map/reduce_scatter | solution.py:642
  1092.4 347.1 %reduce-scatter.35.cloned.1.call-start = ((), (), s32[]{:S(2)}) async-start(), calls=%async_computation.32 | async-start | bytes 2359296 | tf_op jit(solution)/shard_map/reduce_scatter | solution.py:648
  1099.0 385.6 %reduce-scatter.33.cloned.1.call-start = ((), (), s32[]{:S(2)}) async-start(), calls=%async_computation.31 | async-start | bytes 2359296 | tf_op jit(solution)/shard_map/reduce_scatter | solution.py:645
  1105.7 423.7 %reduce-scatter.31.cloned.1.call-start = ((), (), s32[]{:S(2)}) async-start(), calls=%async_computation.30 | async-start | bytes 2359296 | tf_op jit(solution)/shard_map/reduce_scatter | solution.py:644
  1112.0 552.0 %all-reduce.9.cloned.1.call-start = ((), (), s32[]{:S(2)}) async-start(), calls=%async_computation.38 | async-start | bytes 151552 | tf_op jit(solution)/shard_map/psum | solution.py:607
  (42 other events, 1845.3 us)
Sparse Core Ops, SparseCore 0:
  11.5 79.2 all-gather.10
  92.7 24.5 all-gather.14
  144.3 23.4 all-gather.16
  217.6 144.1 reduce-scatter.18
  363.5 26.2 all-gather.22
  392.0 78.0 all-gather.18
  471.9 26.3 all-gather.20
  500.2 25.1 all-gather.24
  526.9 78.0 all-gather.26
  626.4 145.3 reduce-scatter.22
  773.9 77.8 reduce-scatter.20
  856.7 78.5 all-gather.28
  1017.6 35.2 reduce-scatter.42
  1055.8 34.0 reduce-scatter.44
  1092.1 76.7 reduce-scatter.24
  1172.7 45.1 reduce-scatter.40
  1221.8 44.6 reduce-scatter.36
  1270.5 44.7 reduce-scatter.38
  1318.8 35.9 reduce-scatter.28
  1358.6 35.9 reduce-scatter.26
  1398.4 41.1 reduce-scatter.34
  1443.4 41.0 reduce-scatter.32
  1488.3 41.1 reduce-scatter.30
  1537.6 126.3 all-reduce.8
  (1 shorter events, 23.3 us)

commit v2 on v1

v2 whole, which is shorter than its diff:
```python
import functools
import jax
import jax.numpy as jnp
from jax import lax
from jax.experimental import pallas as pl
from jax.experimental.pallas import tpu as pltpu
from jax.sharding import PartitionSpec as P

DK = 128
DV = 256
SLOT = 1024
LANES = 128
BLOCK = 256
HEADS = 2
WIDE_K = HEADS * DK
WIDE_V = HEADS * DV
WIDTH = 2 * WIDE_K + 2 * WIDE_V + LANES
F32 = jnp.float32
BF16 = jnp.bfloat16


def dot(left, right, dim_left, dim_right):
    return lax.dot_general(
        left, right, (((dim_left,), (dim_right,)), ((), ())), preferred_element_type=F32
    )


def halves(value):
    high = value.astype(BF16)
    return high, (value - high.astype(F32)).astype(BF16)


def mm(left, right, dim_left=1, dim_right=0):
    left_high, left_low = halves(left)
    right_high, right_low = halves(right)
    return (
        dot(left_high, right_high, dim_left, dim_right)
        + dot(left_high, right_low, dim_left, dim_right)
        + dot(left_low, right_high, dim_left, dim_right)
    )


def mm_full(left, right, dim_left, dim_right):
    return lax.dot_general(
        left,
        right,
        (((dim_left,), (dim_right,)), ((), ())),
        preferred_element_type=F32,
        precision=lax.Precision.HIGHEST,
    )


def sigmoid(value):
    return 1.0 / (1.0 + jnp.exp(-value))


def softplus(value):
    return jnp.maximum(value, 0.0) + jnp.log1p(jnp.exp(-jnp.abs(value)))


def valid_rows(first, count, start, end):
    position = first + lax.broadcasted_iota(jnp.int32, (count, 1), 0)
    return jnp.where((position >= start) & (position < end), 1.0, 0.0).astype(F32)


def convolve(extended, taps, count):
    total = taps[0:1, :] * extended[5 : 5 + count]
    for offset in range(1, 4):
        total = total + taps[offset : offset + 1, :] * extended[5 + offset : 5 + offset + count]
    return total


def unit_scale(value):
    return lax.rsqrt(jnp.sum(value * value, -1, keepdims=True) + 1e-06)


def triangle(size):
    row = lax.broadcasted_iota(jnp.int32, (size, size), 0)
    column = lax.broadcasted_iota(jnp.int32, (size, size), 1)
    return row, column


def lower_ones(size):
    row, column = triangle(size)
    return jnp.where(row >= column, 1.0, 0.0).astype(F32)


def inverses(systems, size):
    row, column = triangle(size)
    differ = jnp.bitwise_xor(row, column)
    eye = jnp.where(differ == 0, 1.0, 0.0).astype(F32)
    found = [eye - jnp.where(differ == 1, system, 0.0) for system in systems]
    width = 2
    while width < size:
        mask = (differ >= width) & (differ < 2 * width)
        parts = [jnp.where(mask, system, 0.0) for system in systems]
        middle = [mm(f, p) for f, p in zip(found, parts)]
        found = [f - mm(m, f) for f, m in zip(found, middle)]
        width *= 2
    return found


def gather_inputs(first, start, end, refs, heads, block):
    pre_q, pre_k, pre_v, pre_ab, halo_q, halo_k, halo_v, taps_q, taps_k, taps_v, rate, bias = refs
    valid = valid_rows(first, block, start, end)
    halo_valid = valid_rows(first - 8, 8, start, end)
    ext_q = jnp.concatenate([halo_q[...] * halo_valid, pre_q[...] * valid], 0)
    ext_k = jnp.concatenate([halo_k[...] * halo_valid, pre_k[...] * valid], 0)
    ext_v = jnp.concatenate([halo_v[...] * halo_valid, pre_v[...] * valid], 0)
    conv_q = convolve(ext_q, taps_q[...], block)
    conv_k = convolve(ext_k, taps_k[...], block)
    conv_v = convolve(ext_v, taps_v[...], block)
    both = pre_ab[...]
    shifted = both + bias[...]
    decay = rate[...] * softplus(shifted) * valid
    strength = sigmoid(both) * valid
    ones = lower_ones(block)
    cum = mm_full(ones, decay, 1, 0)
    cum_rows = mm_full(decay, ones, 0, 1)
    return dict(
        valid=valid, ext=(ext_q, ext_k, ext_v), conv=(conv_q, conv_k, conv_v), shifted=shifted,
        decay=decay, strength=strength, ones=ones, cum=cum, cum_rows=cum_rows,
    )


def head_operands(common, head, heads, block):
    conv_q, conv_k, conv_v = common["conv"]
    keys = slice(head * DK, (head + 1) * DK)
    vals = slice(head * DV, (head + 1) * DV)
    u_q, u_k, u_v = conv_q[:, keys], conv_k[:, keys], conv_v[:, vals]
    s_q, s_k, s_v = sigmoid(u_q), sigmoid(u_k), sigmoid(u_v)
    y_q, y_k = u_q * s_q, u_k * s_k
    n_q, n_k = unit_scale(y_q), unit_scale(y_k)
    cum = common["cum"][:, head : head + 1]
    cum_row = common["cum_rows"][head : head + 1, :]
    last = common["cum"][block - 1 : block, head : head + 1]
    spread = jnp.exp(jnp.minimum(cum - cum_row, 0.0))
    return dict(
        u=(u_q, u_k, u_v), s=(s_q, s_k, s_v), n=(n_q, n_k), unit=(y_q * n_q, y_k * n_k),
        q=y_q * (n_q * DK ** (-0.5)), k=y_k * (n_k * common["valid"]), v=u_v * s_v,
        beta=common["strength"][:, heads + head : heads + head + 1],
        growth=jnp.exp(cum), remain=jnp.exp(last - cum), whole=jnp.exp(last), spread=spread,
    )


def forward_kernel(heads, block, bounds, pre_q, pre_k, pre_v, pre_g, pre_ab, halo_q, halo_k, halo_v,
                   taps_q, taps_k, taps_v, rate, bias, gain, mixed, out, states, deltas, solves, state):
    row, step = pl.program_id(0), pl.program_id(1)

    @pl.when(step == 0)
    def _():
        state[...] = jnp.zeros_like(state)

    refs = (pre_q, pre_k, pre_v, pre_ab, halo_q, halo_k, halo_v, taps_q, taps_k, taps_v, rate, bias)
    common = gather_inputs(step * block, bounds[0, row], bounds[1, row], refs, heads, block)
    ops = [head_operands(common, head, heads, block) for head in range(heads)]
    at, to = triangle(block)
    systems = [jnp.where(at > to, o["beta"] * o["spread"] * mm(o["k"], o["k"], 1, 1), 0.0) for o in ops]
    found = inverses(systems, block)
    for head, o in enumerate(ops):
        vals = slice(head * DV, (head + 1) * DV)
        old = state[head]
        states[head] = old.astype(states.dtype)
        source = o["beta"] * o["v"] - (o["beta"] * o["growth"]) * mm(o["k"], old)
        delta = mm(found[head], source)
        scores = jnp.where(at >= to, o["spread"] * mm(o["q"], o["k"], 1, 1), 0.0)
        emitted = o["growth"] * mm(o["q"], old) + mm(scores, delta)
        state[head] = o["whole"] * old + mm(o["k"] * o["remain"], delta, 0, 0)
        solves[head] = found[head].astype(solves.dtype)
        deltas[:, vals] = delta.astype(deltas.dtype)
        out[:, vals] = emitted.astype(out.dtype)
        scale = lax.rsqrt(jnp.mean(emitted * emitted, -1, keepdims=True) + 1e-05)
        gate = pre_g[:, vals]
        mixed[:, vals] = (
            emitted * scale * gain[...] * (gate * sigmoid(gate)) * common["valid"]
        ).astype(mixed.dtype)


def backward_kernel(heads, block, steps, bounds, pre_q, pre_k, pre_v, pre_g, pre_ab, halo_q, halo_k, halo_v,
                    taps_q, taps_k, taps_v, rate, bias, gain, out, states, deltas, solves, grad,
                    d_pre, d_taps_q, d_taps_k, d_taps_v, d_small, d_gain,
                    d_state, next_q, next_k, next_v):
    d_q = d_pre.at[:, 0:WIDE_K]
    d_k = d_pre.at[:, WIDE_K : 2 * WIDE_K]
    d_v = d_pre.at[:, 2 * WIDE_K : 2 * WIDE_K + WIDE_V]
    d_g = d_pre.at[:, 2 * WIDE_K + WIDE_V : 2 * WIDE_K + 2 * WIDE_V]
    d_ab = d_pre.at[:, 2 * WIDE_K + 2 * WIDE_V : WIDTH]
    row, back = pl.program_id(0), pl.program_id(1)
    step = steps - 1 - back

    @pl.when((row == 0) & (back == 0))
    def _():
        for ref in (d_taps_q, d_taps_k, d_taps_v, d_small, d_gain):
            ref[...] = jnp.zeros_like(ref)

    @pl.when(back == 0)
    def _():
        for ref in (d_state, next_q, next_k, next_v):
            ref[...] = jnp.zeros_like(ref)

    refs = (pre_q, pre_k, pre_v, pre_ab, halo_q, halo_k, halo_v, taps_q, taps_k, taps_v, rate, bias)
    common = gather_inputs(step * block, bounds[0, row], bounds[1, row], refs, heads, block)
    valid = common["valid"]
    at, to = triangle(block)
    lane = lax.broadcasted_iota(jnp.int32, (block, LANES), 1)
    ones_cols = jnp.ones((block, LANES), BF16)
    d_cum = jnp.zeros((block, LANES), F32)
    d_last = jnp.zeros((1, LANES), F32)
    d_beta = jnp.zeros((block, LANES), F32)
    du_q, du_k, du_v = [], [], []
    gain_sum = jnp.zeros((1, DV), F32)
    for head in range(heads):
        o = head_operands(common, head, heads, block)
        vals = slice(head * DV, (head + 1) * DV)
        q, k, v, beta, growth, remain, whole, spread = (
            o[name] for name in ("q", "k", "v", "beta", "growth", "remain", "whole", "spread"))
        emitted = out[:, vals].astype(F32)
        scale = lax.rsqrt(jnp.mean(emitted * emitted, -1, keepdims=True) + 1e-05)
        unit = emitted * scale
        gate = pre_g[:, vals]
        s_g = sigmoid(gate)
        d_mixed = grad[:, vals].astype(F32) * valid
        d_g[:, vals] = (d_mixed * unit * gain[...] * (s_g * (1.0 + gate * (1.0 - s_g)))).astype(d_g.dtype)
        part = d_mixed * (gate * s_g)
        gain_sum = gain_sum + jnp.sum(part * unit, 0, keepdims=True)
        weighted = part * gain[...]
        d_out = scale * (weighted - unit * jnp.mean(weighted * unit, -1, keepdims=True))
        old = states[head].astype(F32)
        delta = deltas[:, vals]
        solve = solves[head]
        d_new = d_state[head]
        q_k = mm(q, k, 1, 1)
        k_k = mm(k, k, 1, 1)
        scores = jnp.where(at >= to, spread * q_k, 0.0)
        linked = jnp.where(at > to, spread * k_k, 0.0)
        k_s = mm(k, old)
        q_s = mm(q, old)
        k_rem = k * remain
        d_delta = mm(scores, d_out, 0, 0) + mm(k_rem, d_new)
        d_source = mm(solve, d_delta, 0, 0)
        d_system = -mm(d_source, delta, 1, 1)
        d_scores = mm(d_out, delta, 1, 1)
        d_qk = jnp.where(at >= to, d_scores * spread, 0.0)
        by_link = d_system * linked
        d_kk = jnp.where(at > to, beta * d_system * spread, 0.0)
        edge, edge_low = halves(d_scores * scores + beta * by_link)
        d_query = growth * mm(d_out, old, 1, 1) + mm(d_qk, k)
        back_state = mm(delta, d_new, 1, 1)
        d_key = (
            mm((beta * growth) * d_source, old, 1, 1) * (-1.0)
            + mm(d_qk, q, 0, 0)
            + mm(d_kk, k)
            + mm(d_kk, k, 0, 0)
            + remain * back_state
        )
        d_value = beta * d_source
        lose = jnp.sum(k_rem * back_state, -1, keepdims=True)
        pull = jnp.sum(d_source * k_s, -1, keepdims=True)
        grow = growth * (jnp.sum(d_out * q_s, -1, keepdims=True) - beta * pull)
        d_b = jnp.sum(d_source * v, -1, keepdims=True) - growth * pull + jnp.sum(by_link, -1, keepdims=True)
        cut = (
            dot(edge, ones_cols, 1, 0) - dot(edge, ones_cols, 0, 0)
            + dot(edge_low, ones_cols, 1, 0) - dot(edge_low, ones_cols, 0, 0)
        )
        d_cum = jnp.where(lane == head, cut + (grow - lose), d_cum)
        d_beta = jnp.where(lane == heads + head, d_b, d_beta)
        total = jnp.sum(lose, keepdims=True) + whole * jnp.sum(old * d_new, keepdims=True)
        d_last = jnp.where(lane[0:1] == head, total, d_last)
        d_state[head] = (
            whole * d_new + mm(q, growth * d_out, 0, 0) - mm(k * (beta * growth), d_source, 0, 0)
        )
        unit_q, unit_k = o["unit"]
        n_q, n_k = o["n"]
        d_unit = d_query * DK ** (-0.5)
        d_yq = n_q * (d_unit - unit_q * jnp.sum(unit_q * d_unit, -1, keepdims=True))
        d_unit = d_key * valid
        d_yk = n_k * (d_unit - unit_k * jnp.sum(unit_k * d_unit, -1, keepdims=True))
        for store, d_y, u, s in zip((du_q, du_k, du_v), (d_yq, d_yk, d_value), o["u"], o["s"]):
            store.append(d_y * (s * (1.0 + u * (1.0 - s))))
    d_decay = mm_full(common["ones"], d_cum, 0, 0) + d_last
    slope = d_decay * rate[...] * sigmoid(common["shifted"]) * valid
    strength = common["strength"]
    d_pre_b = d_beta * strength * (1.0 - strength)
    d_ab[...] = (slope + d_pre_b).astype(d_ab.dtype)
    d_small[0:1, :] += jnp.sum(d_decay * common["decay"], 0, keepdims=True)
    d_small[1:2, :] += jnp.sum(slope, 0, keepdims=True)
    d_gain[0:1, :] += gain_sum
    for store, ext, taps, d_taps, later, target in zip(
        (du_q, du_k, du_v), common["ext"], (taps_q, taps_k, taps_v), (d_taps_q, d_taps_k, d_taps_v),
        (next_q, next_k, next_v), (d_q, d_k, d_v),
    ):
        du = jnp.concatenate(store, 1) if heads > 1 else store[0]
        longer = jnp.concatenate([du, later[...]], 0)
        later[...] = du[0:8]
        total = taps[3:4, :] * du
        for offset in range(3):
            total = total + taps[offset : offset + 1, :] * longer[3 - offset : 3 - offset + block]
        target[...] = (total * valid).astype(target.dtype)
        for offset in range(4):
            d_taps[offset : offset + 1, :] += jnp.sum(du * ext[5 + offset : 5 + offset + block], 0, keepdims=True)


def pre_specs(place):
    def tile(width, column):
        return pl.BlockSpec((None, BLOCK, width), lambda r, c, *_: (r, place(c), column))

    def halo(width, column):
        return pl.BlockSpec(
            (None, 8, width),
            lambda r, c, *_: (r, jnp.maximum(place(c) * (BLOCK // 8) - 1, 0), column),
        )

    def fixed(rows, width):
        return pl.BlockSpec((rows, width), lambda r, c, *_: (0, 0))

    return [
        tile(WIDE_K, 0), tile(WIDE_K, 1), tile(WIDE_V, 1), tile(WIDE_V, 2),
        tile(LANES, (WIDTH - LANES) // LANES),
        halo(WIDE_K, 0), halo(WIDE_K, 1), halo(WIDE_V, 1),
        fixed(8, WIDE_K), fixed(8, WIDE_K), fixed(8, WIDE_V),
        fixed(1, LANES), fixed(1, LANES), fixed(1, DV),
    ]


def mixer_forward(bounds, pre, small):
    rows = pre.shape[0]
    steps = SLOT // BLOCK
    tile_v = pl.BlockSpec((None, BLOCK, WIDE_V), lambda r, c, *_: (r, c, 0))
    return pl.pallas_call(
        functools.partial(forward_kernel, HEADS, BLOCK),
        grid_spec=pltpu.PrefetchScalarGridSpec(
            num_scalar_prefetch=1,
            grid=(rows, steps),
            in_specs=pre_specs(lambda c: c),
            out_specs=[
                tile_v, tile_v,
                pl.BlockSpec((None, None, HEADS, DK, DV), lambda r, c, *_: (r, c, 0, 0, 0)),
                tile_v,
                pl.BlockSpec((None, None, HEADS, BLOCK, BLOCK), lambda r, c, *_: (r, c, 0, 0, 0)),
            ],
            scratch_shapes=[pltpu.VMEM((HEADS, DK, DV), F32)],
        ),
        out_shape=[
            jax.ShapeDtypeStruct((rows, SLOT, WIDE_V), BF16),
            jax.ShapeDtypeStruct((rows, SLOT, WIDE_V), F32),
            jax.ShapeDtypeStruct((rows, steps, HEADS, DK, DV), F32),
            jax.ShapeDtypeStruct((rows, SLOT, WIDE_V), F32),
            jax.ShapeDtypeStruct((rows, steps, HEADS, BLOCK, BLOCK), F32),
        ],
        cost_estimate=pl.CostEstimate(
            flops=10**10 * rows, bytes_accessed=2 * 10**7 * rows, transcendentals=10**7 * rows),
        name="mixer_forward",
    )(bounds, *[pre] * 8, *small)


def mixer_backward(bounds, pre, small, saved, grad):
    rows = pre.shape[0]
    steps = SLOT // BLOCK

    def tile(width):
        return pl.BlockSpec((None, BLOCK, width), lambda r, c, *_: (r, steps - 1 - c, 0))

    def fixed(rows, width):
        return pl.BlockSpec((rows, width), lambda r, c, *_: (0, 0))

    return pl.pallas_call(
        functools.partial(backward_kernel, HEADS, BLOCK, steps),
        grid_spec=pltpu.PrefetchScalarGridSpec(
            num_scalar_prefetch=1,
            grid=(rows, steps),
            in_specs=pre_specs(lambda c: steps - 1 - c) + [
                tile(WIDE_V),
                pl.BlockSpec((None, None, HEADS, DK, DV), lambda r, c, *_: (r, steps - 1 - c, 0, 0, 0)),
                tile(WIDE_V),
                pl.BlockSpec((None, None, HEADS, BLOCK, BLOCK), lambda r, c, *_: (r, steps - 1 - c, 0, 0, 0)),
                tile(WIDE_V),
            ],
            out_specs=[
                tile(WIDTH),
                fixed(8, WIDE_K), fixed(8, WIDE_K), fixed(8, WIDE_V), fixed(8, LANES), fixed(8, DV),
            ],
            scratch_shapes=[
                pltpu.VMEM((HEADS, DK, DV), F32),
                pltpu.VMEM((8, WIDE_K), F32), pltpu.VMEM((8, WIDE_K), F32), pltpu.VMEM((8, WIDE_V), F32),
            ],
        ),
        out_shape=[
            jax.ShapeDtypeStruct((rows, SLOT, WIDTH), BF16),
            jax.ShapeDtypeStruct((8, WIDE_K), F32),
            jax.ShapeDtypeStruct((8, WIDE_K), F32),
            jax.ShapeDtypeStruct((8, WIDE_V), F32),
            jax.ShapeDtypeStruct((8, LANES), F32),
            jax.ShapeDtypeStruct((8, DV), F32),
        ],
        cost_estimate=pl.CostEstimate(
            flops=10**10 * rows, bytes_accessed=2 * 10**7 * rows, transcendentals=10**7 * rows),
        name="mixer_backward",
    )(bounds, *[pre] * 8, *small, *saved, grad)


def matmul(left, right):
    return jnp.dot(left, right, preferred_element_type=F32)


def matmul_t(left, right):
    return lax.dot_general(left, right, (((1,), (1,)), ((), ())), preferred_element_type=F32)


def inner(left, right):
    return lax.dot_general(left, right, (((0,), (0,)), ((), ())), preferred_element_type=F32)


def norm_backward(grad_normed, inputs, scale, gain):
    unit = inputs * scale
    weighted = grad_normed * gain
    grad_gain = jnp.sum(grad_normed * unit, 0)
    grad_inputs = scale * (weighted - unit * jnp.mean(weighted * unit, -1, keepdims=True))
    return (grad_inputs, grad_gain)


def swap(value, axis, size, mask):
    return lax.ppermute(value, axis, [(i, i ^ mask) for i in range(size)])


def relative_order(devices):
    return list(range(0, devices, 2)) + list(range(1, devices, 2))


def relative_matrix(width, devices, me):
    block = width // devices
    order = jnp.array(relative_order(devices), jnp.int32)
    column = jnp.arange(width, dtype=jnp.int32)
    source = jnp.bitwise_xor(jnp.repeat(order, block), me) * block + column % block
    return (jnp.arange(width, dtype=jnp.int32)[:, None] == source[None, :]).astype(BF16)


def scatter_sum(product, left, devices):
    half = left.shape[1] // 2
    block = half * 2 // devices
    got = swap(product(left[:, half:]).astype(BF16), "dp", devices, 1)
    keep = product(left[:, :half]) + got.astype(F32)
    count, stride = devices // 2, 2
    lead = keep.shape[:-2]
    while count > 1:
        ways = min(4, count)
        shaped = keep.reshape(lead + (count // ways, ways, block, keep.shape[-1]))
        keep = shaped[..., :, 0, :, :]
        for way in range(1, ways):
            sent = shaped[..., :, way, :, :].astype(BF16)
            keep = keep + swap(sent, "dp", devices, way * stride).astype(F32)
        count //= ways
        stride *= ways
        keep = keep.reshape(lead + (count * block, keep.shape[-1]))
    return keep


def shards(
    tokens, lengths, starts, norm_one, w_query, w_key, w_value, w_gating, w_decay, w_strength,
    filter_query, filter_key, filter_value, decay_log, decay_bias, head_gain, w_output, norm_two,
    w_gate, w_up, w_down, cotangent,
):
    rank, me = lax.axis_index("tensor"), lax.axis_index("dp")
    ranks, devices = lax.axis_size("tensor"), lax.axis_size("dp")
    tok_dev, width = tokens.shape
    units = w_gate.shape[1]
    wide = -(-units // LANES) * LANES
    half = rank % 2
    row = rank // 2
    slot_pos = jnp.arange(SLOT, dtype=jnp.int32)
    row_mask = (
        (slot_pos[None, :] >= starts[:, None]) & (slot_pos[None, :] < (starts + lengths)[:, None])
    ).astype(F32)
    mask = lax.dynamic_slice_in_dim(row_mask.reshape(-1), rank * tok_dev, tok_dev)[:, None]
    bounds = lax.dynamic_slice_in_dim(jnp.stack([starts, starts + lengths]), row, 1, 1)

    def both_halves(mine, other):
        return jnp.where(half == 0, jnp.concatenate([mine, other], 0), jnp.concatenate([other, mine], 0))

    def exchange(value):
        return swap(value, "tensor", ranks, 1)

    inputs = tokens.astype(F32)
    scale_one = lax.rsqrt(jnp.mean(inputs * inputs, -1, keepdims=True) + 1e-05)
    normed_one = (inputs * scale_one * norm_one).astype(BF16)
    row_one = both_halves(normed_one, exchange(normed_one))

    spare = jnp.zeros((w_query.shape[0], LANES - 2 * HEADS), BF16)
    packed = jnp.concatenate([w_query, w_key, w_value, w_gating, w_decay, w_strength, spare], 1)
    first = lax.ppermute(packed, "tensor", [(1, 0), (3, 1), (2, 3), (0, 2)])
    second = lax.ppermute(packed, "tensor", [(1, 2), (2, 1)])
    lower = jnp.where(rank == 0, packed, jnp.where(rank == 1, second, first))
    upper = jnp.where(rank == 3, packed, jnp.where(rank == 2, second, first))
    mixer_weights = [lax.all_gather(w, "dp", axis=0, tiled=True) for w in (lower, upper)]

    def gather(value):
        whole = lax.all_gather(value, ("tensor", "dp"), axis=0, tiled=True)
        return whole.reshape(ranks, width, value.shape[1])

    pad = ((0, 0), (0, wide - units))
    out_t = gather(w_output.T)
    gate_w = gather(jnp.pad(w_gate, pad))
    up_w = gather(jnp.pad(w_up, pad))
    down_t = gather(jnp.pad(w_down.T, pad))

    def small_of(shard):
        def taps(values, columns):
            return jnp.pad(lax.dynamic_slice_in_dim(values, shard * columns, columns, 1), ((0, 4), (0, 0)))

        log = lax.dynamic_slice_in_dim(decay_log, shard * HEADS, HEADS)
        bias = lax.dynamic_slice_in_dim(decay_bias, shard * HEADS, HEADS)
        return (
            taps(filter_query, WIDE_K), taps(filter_key, WIDE_K), taps(filter_value, WIDE_V),
            jnp.pad(-jnp.exp(log), (0, LANES - HEADS))[None],
            jnp.pad(bias, (0, LANES - HEADS))[None],
            head_gain[None],
        )

    shard_ids = [2 * half, 2 * half + 1]
    smalls = [small_of(s) for s in shard_ids]
    pres = [matmul(row_one, w)[None] for w in mixer_weights]
    saves, own, got = [], [], []
    for pre, small in zip(pres, smalls):
        mixed, *saved = mixer_forward(bounds, pre, small)
        saves.append(saved)
        own.append(lax.dynamic_slice_in_dim(mixed[0], half * tok_dev, tok_dev))
        got.append(exchange(lax.dynamic_slice_in_dim(mixed[0], (1 - half) * tok_dev, tok_dev)))
    mixed = [jnp.where(half == 0, a, b) for a, b in zip(own + got, got + own)]
    attention = matmul_t(mixed[0], out_t[0])
    for part, weight in zip(mixed[1:], out_t[1:]):
        attention = attention + matmul_t(part, weight)
    middle = inputs + attention
    scale_two = lax.rsqrt(jnp.mean(middle * middle, -1, keepdims=True) + 1e-05)
    normed_two = (middle * scale_two * norm_two).astype(BF16)

    relative = relative_matrix(width, devices, me)

    def to_relative(value):
        return matmul(value, relative).astype(BF16)

    residual_grad = cotangent.astype(F32) * mask
    feed_grad = residual_grad.astype(BF16)
    feed_rel = to_relative(feed_grad)
    two_rel = to_relative(normed_two)
    feed = None
    two_grad = None
    hiddens, gate_grads, up_grads = [], [], []
    for t in range(ranks):
        gate_pre = matmul(normed_two, gate_w[t])
        up_pre = matmul(normed_two, up_w[t])
        s = jax.nn.sigmoid(gate_pre)
        hidden = (gate_pre * s * up_pre).astype(BF16)
        hidden_grad = matmul(feed_grad, down_t[t])
        gate_grad = (hidden_grad * up_pre * s * (1.0 + gate_pre * (1.0 - s))).astype(BF16)
        up_grad = (hidden_grad * gate_pre * s).astype(BF16)
        hiddens.append(hidden)
        gate_grads.append(gate_grad)
        up_grads.append(up_grad)
        part = matmul_t(hidden, down_t[t])
        feed = part if feed is None else feed + part
        part = matmul_t(gate_grad, gate_w[t]) + matmul_t(up_grad, up_w[t])
        two_grad = part if two_grad is None else two_grad + part
    block_out = (mask * (middle + feed)).astype(BF16)

    def many(values):
        return lambda left: jnp.stack([inner(left, v) for v in values])

    sum_gate = scatter_sum(many(gate_grads), two_rel, devices)
    sum_up = scatter_sum(many(up_grads), two_rel, devices)
    sum_down = scatter_sum(many(hiddens), feed_rel, devices)

    middle_part, grad_norm_two = norm_backward(two_grad, middle, scale_two, norm_two)
    middle_grad = residual_grad + middle_part
    attention_grad = middle_grad.astype(BF16)
    mixed_grads = []
    for j in range(2):
        sent = matmul(attention_grad, out_t[2 * (1 - half) + j]).astype(BF16)
        kept = matmul(attention_grad, out_t[2 * half + j]).astype(BF16)
        mixed_grads.append(both_halves(kept, exchange(sent))[None])
    sum_out = scatter_sum(many(mixed), to_relative(attention_grad), devices)

    one_rel = to_relative(row_one)
    one_part = None
    mixer_sums, smalls_grads = [], []
    for j in range(2):
        d_pre, *d_small = mixer_backward(bounds, pres[j], smalls[j], saves[j], mixed_grads[j])
        d_pre = d_pre[0]
        smalls_grads.append(d_small)
        mixer_sums.append(scatter_sum(lambda left: inner(left, d_pre), one_rel, devices))
        part = matmul_t(d_pre, mixer_weights[j])
        one_part = part if one_part is None else one_part + part
    one_kept = lax.dynamic_slice_in_dim(one_part, half * tok_dev, tok_dev)
    one_sent = lax.dynamic_slice_in_dim(one_part, (1 - half) * tok_dev, tok_dev)
    one_grad = one_kept + exchange(one_sent.astype(BF16)).astype(F32)
    input_part, grad_norm_one = norm_backward(one_grad, inputs, scale_one, norm_one)
    grad_tokens = middle_grad + input_part

    feeds = jnp.concatenate([sum_gate, sum_up, sum_down, sum_out], -1)
    owned = feeds[rank]
    for mask_z in range(1, ranks):
        owned = owned + swap(feeds[rank ^ mask_z].astype(BF16), "tensor", ranks, mask_z).astype(F32)
    owned_gate = owned[:, :units]
    owned_up = owned[:, wide : wide + units]
    owned_down = owned[:, 2 * wide : 2 * wide + units].T
    owned_out = owned[:, 3 * wide :].T

    low, high = mixer_sums
    first = lax.ppermute(
        jnp.where(rank < 2, high, low).astype(BF16), "tensor", [(0, 1), (1, 3), (3, 2), (2, 0)])
    second = lax.ppermute(jnp.where(rank == 2, high, low).astype(BF16), "tensor", [(2, 1), (1, 2)])
    third = jnp.where(rank == 0, low, jnp.where(rank == 3, high, second.astype(F32)))
    mixer_owned = first.astype(F32) + third

    def place(total, values, columns):
        for shard, value in zip(shard_ids, values):
            total = lax.dynamic_update_slice_in_dim(total, value, shard * columns, total.ndim - 1)
        return total

    pieces = [
        grad_norm_one, grad_norm_two, smalls_grads[0][4][0] + smalls_grads[1][4][0],
        place(jnp.zeros_like(filter_query), [g[0][:4] for g in smalls_grads], WIDE_K),
        place(jnp.zeros_like(filter_key), [g[1][:4] for g in smalls_grads], WIDE_K),
        place(jnp.zeros_like(filter_value), [g[2][:4] for g in smalls_grads], WIDE_V),
        place(jnp.zeros_like(decay_log), [g[3][0, :HEADS] for g in smalls_grads], HEADS),
        place(jnp.zeros_like(decay_bias), [g[3][1, :HEADS] for g in smalls_grads], HEADS),
    ]
    sizes = [p.size for p in pieces]
    length = -(-sum(sizes) // 1024) * 1024
    flat = jnp.concatenate([p.reshape(-1) for p in pieces] + [jnp.zeros((length - sum(sizes),), F32)])
    flat = flat.reshape(-1, LANES)
    bit = 1
    while bit < devices:
        flat = flat + swap(flat, "dp", devices, bit)
        bit *= 2
    bit = 1
    while bit < ranks:
        flat = flat + swap(flat, "tensor", ranks, bit)
        bit *= 2
    flat = flat.reshape(-1)
    summed, at = [], 0
    for piece, size in zip(pieces, sizes):
        summed.append(flat[at : at + size].reshape(piece.shape))
        at += size
    sum_one, sum_two, sum_gain, sum_fq, sum_fk, sum_fv, sum_log, sum_bias = summed
    edges = [WIDE_K, 2 * WIDE_K, 2 * WIDE_K + WIDE_V, WIDTH - LANES, WIDTH - LANES + HEADS]
    return (
        block_out, grad_tokens, sum_one,
        mixer_owned[:, : edges[0]],
        mixer_owned[:, edges[0] : edges[1]],
        mixer_owned[:, edges[1] : edges[2]],
        mixer_owned[:, edges[2] : edges[3]],
        mixer_owned[:, edges[3] : edges[4]],
        mixer_owned[:, edges[4] : edges[4] + HEADS],
        sum_fq, sum_fk, sum_fv, sum_log, sum_bias, sum_gain,
        owned_out, sum_two, owned_gate, owned_up, owned_down,
    )


def solution(mesh):
    placed = (
        P(("dp", "tensor"), None),
        P("dp"),
        P("dp"),
        P(),
        P("dp", "tensor"),
        P("dp", "tensor"),
        P("dp", "tensor"),
        P("dp", "tensor"),
        P("dp", "tensor"),
        P("dp", "tensor"),
        P(),
        P(),
        P(),
        P(),
        P(),
        P(),
        P("tensor", "dp"),
        P(),
        P("dp", "tensor"),
        P("dp", "tensor"),
        P("tensor", "dp"),
        P(("dp", "tensor"), None),
    )
    return jax.shard_map(
        shards,
        mesh=mesh,
        in_specs=placed,
        out_specs=(
            P(("dp", "tensor"), None),
            P(("dp", "tensor"), None),
            P(),
            P("dp", "tensor"),
            P("dp", "tensor"),
            P("dp", "tensor"),
            P("dp", "tensor"),
            P("dp", "tensor"),
            P("dp", "tensor"),
            P(),
            P(),
            P(),
            P(),
            P(),
            P(),
            P("tensor", "dp"),
            P(),
            P("dp", "tensor"),
            P("dp", "tensor"),
            P("tensor", "dp"),
        ),
        check_vma=False,
    )
```

time: 1690 us -> 947 us (0.56)
  waiting for transfers between devices: 1270 us -> 426 us
  local copies, waits for them, and re-layouts: 20.8 us -> 80.3 us
  other arithmetic: 23.7 us -> 67.9 us
  starting transfers between devices: 2.06 us -> 44.9 us
  blocking collectives: 36.2 us -> 0 us
  matrix products: 183 us -> 164 us
    reduce_scatter x12 -> x0, waiting for transfers between devices: 764 us -> none  [the longest x1 144 us: shards(): lax.psum_scatter(jnp.dot(mixed, full_output, preferred_element_type=jnp.f...]
    ppermute x0 -> x42, waiting for transfers between devices: none -> 220 us  [the longest x38 201 us: swap(): return lax.ppermute(value, axis, [(i, i ^ mask) for i in range(size)])]
    all_gather x10 -> x6, waiting for transfers between devices: 370 us -> 204 us  [the longest x4 199 us: gather(): whole = lax.all_gather(value, ('tensor', 'dp'), axis=0, tiled=True)]
    psum x1 -> x0, waiting for transfers between devices: 134 us -> none  [shards(): lax.psum((grad_norm_one, grad_norm_two, pulled[11], placed_query, placed_...]
    ppermute x0 -> x42, starting transfers between devices: none -> 44.6 us  [the longest x38 38.1 us: swap(): return lax.ppermute(value, axis, [(i, i ^ mask) for i in range(size)])]
    all_gather x4 -> x0, blocking collectives: 36.2 us -> none  [the longest x1 9.81 us: shards(): lax.all_gather(w_key, 'dp', axis=0, tiled=True)]
    reshape x0 -> x9, local copies, waits for them, and re-layouts: none -> 35.6 us  [the longest x6 33.7 us: scatter_sum(): shaped = keep.reshape(lead + (count // ways, ways, block, keep.shape[-1]))]
    another operation x1 -> x11, other arithmetic: 0.57 us -> 22.7 us  [shards(): bounds = jnp.stack([starts, starts + lengths])]
  transfers between devices with their start and end apart: 25 -> 48, of which waited for: 22 -> 24; matrix products, arithmetic and copies ran while one was open for 10% -> 25% of each run, Pallas kernels for 4% -> 15%
where the time goes in v2:
time: 947 us; the launch traced here: 936 us
  waiting for transfers between devices  426 us (45%)
  matrix products  164 us (17%)
  Pallas kernels  136 us (14%)
  local copies, waits for them, and re-layouts  80.3 us (8%)
  other arithmetic  67.9 us (7%)
  starting transfers between devices  44.9 us (5%)
  between operations  16.4 us (2%)
    ppermute x38, waiting for transfers between devices, swap(): return lax.ppermute(value, axis, [(i, i ^ mask) for i in range(size)])  201 us
    all_gather x4, waiting for transfers between devices, gather(): whole = lax.all_gather(value, ('tensor', 'dp'), axis=0, tiled=True)  199 us
    pallas_call x2, Pallas kernels, mixer_backward(): pl.pallas_call(functools.partial(backward_kernel, HEADS, BLOCK, steps), g...  72 us
    dot_general x22, matrix products, matmul(): return jnp.dot(left, right, preferred_element_type=F32)  68 us
    pallas_call x2, Pallas kernels, mixer_forward(): pl.pallas_call(functools.partial(forward_kernel, HEADS, BLOCK), grid_spec...  64.2 us
    dot_general x36, matrix products, inner(): lax.dot_general(left, right, (((0,), (0,)), ((), ())), preferred_element_...  56.8 us
    dot_general x18, matrix products, matmul_t(): lax.dot_general(left, right, (((1,), (1,)), ((), ())), preferred_element_...  39.2 us
    ppermute x38, starting transfers between devices, swap(): return lax.ppermute(value, axis, [(i, i ^ mask) for i in range(size)])  38.1 us
  transfers between devices with their start and end apart: 48, of which 24 were waited for; matrix products, arithmetic and copies ran while one was open for 25% of the time, Pallas kernels for 15%

profile of v2, /device:TPU:8, one launch (start us, length us, event | category | flops | bytes accessed | tf_op | source)
XLA Modules:
  0.0 935.8 jit_solution(11049286273031812520)
XLA Ops:
  15.9 19.0 %collective-permute-done.1 = bf16[128,1664]{0,1:T(8,128)(2,1)S(1)} collective-permute-done((bf16[128,1664]{0,1:T(8,128)(2,1)S(1)}, bf16[128,1664]{0,1:T(8,128)(2,1)S(1)}, u32[]{:S(2)}, u32[]{:S(2)}) %collective-permute-start.1) | collective-permute-done | bytes 426016 | tf_op jit(solution)/shard_map/ppermute | solution.py:490
  49.6 15.0 %collective-permute-done = bf16[512,1024]{1,0:T(8,128)(2,1)} collective-permute-done((bf16[512,1024]{1,0:T(8,128)(2,1)S(1)}, bf16[512,1024]{1,0:T(8,128)(2,1)}, u32[]{:S(2)}, u32[]{:S(2)}) %collective-permute-start) | collective-permute-done | bytes 1048608 | tf_op jit(solution)/shard_map/ppermute | solution.py:422
  70.1 9.3 convolution_bitcast_fusion.pre_q.pre_k.pre_v.pre_g.pre_ab.halo_q.halo_k.halo_v
  79.4 32.2 %mixer_forward.3 = (bf16[1,1024,512]{2,1,0:T(8,128)(2,1)}, f32[1,1024,512]{2,1,0:T(8,128)}, f32[1,4,2,128,256]{4,3,2,1,0:T(8,128)}, f32[1,1024,512]{2,1,0:T(8,128)}, f32[1,4,2,256,256]{4,3,2,1,0:T(8,128)}) custom-call(s32[2,1]{1,0:T(2,128)} %constant_dynamic-slice_fusion.6.bounds, ...), custom_call_target="tpu_custom_call" | custom-call | flops 10000000000 | bytes 20000000 | tf_op jit(solution)/shard_map/mixer_forward/pallas_call | solution.py:329
  113.3 9.4 %convolution_bitcast_fusion.1.pre_q.pre_k.pre_v.pre_g.pre_ab.halo_q.halo_k.halo_v = f32[1,1024,1664]{2,1,0:T(8,128)} fusion(bf16[1024,1664]{0,1:T(8,128)(2,1)} %all-gather.7.cloned.1.call-done, bf16[512,1024]{1,0:T(8,128)(2,1)} %collective-permute-done, bf16[512,1024]{1,0:T(8,128)(2,1)S(1)} %fusion.26, pred[]{:T(512)S(6)} %eq.20), kind=kOutput, calls=%fused_computation.5 | convolution fusion | flops 3499098112 | bytes 12320769 | tf_op jit(solution)/shard_map/dot_general | solution.py:402
  122.7 31.9 %mixer_forward.2 = (bf16[1,1024,512]{2,1,0:T(8,128)(2,1)}, f32[1,1024,512]{2,1,0:T(8,128)}, f32[1,4,2,128,256]{4,3,2,1,0:T(8,128)}, f32[1,1024,512]{2,1,0:T(8,128)}, f32[1,4,2,256,256]{4,3,2,1,0:T(8,128)}) custom-call(s32[2,1]{1,0:T(2,128)} %constant_dynamic-slice_fusion.6.bounds, ...), custom_call_target="tpu_custom_call" | custom-call | flops 10000000000 | bytes 20000000 | tf_op jit(solution)/shard_map/mixer_forward/pallas_call | solution.py:329
  163.7 15.1 %collective-permute-done.3 = bf16[512,512]{1,0:T(8,128)(2,1)S(1)} collective-permute-done((bf16[512,512]{1,0:T(8,128)(2,1)S(1)}, bf16[512,512]{1,0:T(8,128)(2,1)S(1)}, u32[]{:S(2)}, u32[]{:S(2)}) %collective-permute-start.3) | collective-permute-done | bytes 524320 | tf_op jit(solution)/shard_map/ppermute | solution.py:422
  180.2 6.7 copy.67
  195.7 64.5 %all-gather.13.cloned.1.call-done = bf16[4096,768]{0,1:T(8,128)(2,1)} async-done(((bf16[128,768]{0,1:T(8,128)(2,1)}), bf16[4096,768]{0,1:T(8,128)(2,1)}) %all-gather.13.cloned.1.call-update) | async-done | bytes 6291472 | tf_op jit(solution)/shard_map/all_gather | solution.py:496
  267.8 72.5 %all-gather.15.cloned.1.call-done = bf16[4096,768]{0,1:T(8,128)(2,1)} async-done(((bf16[128,768]{0,1:T(8,128)(2,1)}), bf16[4096,768]{0,1:T(8,128)(2,1)}) %all-gather.15.cloned.1.call-update) | async-done | bytes 6291472 | tf_op jit(solution)/shard_map/all_gather | solution.py:496
  359.7 60.8 %all-gather.17.cloned.1.call-done = bf16[4096,768]{0,1:T(8,128)(2,1)} async-done(((bf16[128,768]{0,1:T(8,128)(2,1)}), bf16[4096,768]{0,1:T(8,128)(2,1)}) %all-gather.17.cloned.1.call-update) | async-done | bytes 6291472 | tf_op jit(solution)/shard_map/all_gather | solution.py:496
  515.9 35.9 %mixer_backward.3 = (bf16[1,1024,1664]{2,1,0:T(8,128)(2,1)}, f32[8,256]{1,0:T(8,128)}, f32[8,256]{1,0:T(8,128)}, f32[8,512]{1,0:T(8,128)}, f32[8,128]{1,0:T(8,128)}, /*index=5*/f32[8,256]{1,0:T(8,128)}) custom-call(s32[2,1]{1,0:T(2,128)} %constant_dynamic-slice_fusion.6.bounds, ...), custom_call_target="tpu_custom_call" | custom-call | flops 10000000000 | bytes 20000000 | tf_op jit(solution)/shard_map/mixer_backward/pallas_call | solution.py:366
  551.9 36.1 %mixer_backward.2 = (bf16[1,1024,1664]{2,1,0:T(8,128)(2,1)}, f32[8,256]{1,0:T(8,128)}, f32[8,256]{1,0:T(8,128)}, f32[8,512]{1,0:T(8,128)}, f32[8,128]{1,0:T(8,128)}, /*index=5*/f32[8,256]{1,0:T(8,128)}) custom-call(s32[2,1]{1,0:T(2,128)} %constant_dynamic-slice_fusion.6.bounds, ...), custom_call_target="tpu_custom_call" | custom-call | flops 10000000000 | bytes 20000000 | tf_op jit(solution)/shard_map/mixer_backward/pallas_call | solution.py:366
  603.7 19.4 %collective-permute-done.7 = bf16[512,1024]{1,0:T(8,128)(2,1)S(1)} collective-permute-done((bf16[512,1024]{1,0:T(8,128)(2,1)S(1)}, bf16[512,1024]{1,0:T(8,128)(2,1)S(1)}, u32[]{:S(2)}, u32[]{:S(2)}) %collective-permute-start.7) | collective-permute-done | bytes 1048608 | tf_op jit(solution)/shard_map/ppermute | solution.py:422
  692.3 9.0 collective-permute-done.16
  702.3 8.1 collective-permute-done.15
  713.4 9.8 %collective-permute-done.20 = bf16[1,128,1664]{1,2,0:T(8,128)(2,1)} collective-permute-done((bf16[1,128,1664]{1,2,0:T(8,128)(2,1)S(1)}, bf16[1,128,1664]{1,2,0:T(8,128)(2,1)}, u32[]{:S(2)}, u32[]{:S(2)}) %collective-permute-start.20) | collective-permute-done | bytes 426016 | tf_op jit(solution)/shard_map/ppermute | solution.py:422
  779.3 6.9 copy.72
  794.3 14.4 %collective-permute-done.30 = bf16[4,1,128,768]{2,3,0,1:T(8,128)(2,1)} collective-permute-done((bf16[4,1,128,768]{2,3,0,1:T(8,128)(2,1)}, bf16[4,1,128,768]{2,3,0,1:T(8,128)(2,1)}, u32[]{:S(2)}, u32[]{:S(2)}) %collective-permute-start.30) | collective-permute-done | bytes 786464 | tf_op jit(solution)/shard_map/ppermute | solution.py:422
  812.2 13.4 %collective-permute-done.29 = bf16[4,1,128,768]{2,3,0,1:T(8,128)(2,1)} collective-permute-done((bf16[4,1,128,768]{2,3,0,1:T(8,128)(2,1)S(1)}, bf16[4,1,128,768]{2,3,0,1:T(8,128)(2,1)}, u32[]{:S(2)}, u32[]{:S(2)}) %collective-permute-start.29) | collective-permute-done | bytes 786464 | tf_op jit(solution)/shard_map/ppermute | solution.py:422
  830.8 11.6 %collective-permute-done.26 = bf16[4,1,128,768]{2,3,0,1:T(8,128)(2,1)S(1)} collective-permute-done((bf16[4,1,128,768]{2,3,0,1:T(8,128)(2,1)S(1)}, bf16[4,1,128,768]{2,3,0,1:T(8,128)(2,1)S(1)}, u32[]{:S(2)}, u32[]{:S(2)}) %collective-permute-start.26) | collective-permute-done | bytes 786464 | tf_op jit(solution)/shard_map/ppermute | solution.py:422
  842.4 14.0 %collective-permute-done.25 = bf16[4,1,128,768]{2,3,0,1:T(8,128)(2,1)S(1)} collective-permute-done((bf16[4,1,128,768]{2,3,0,1:T(8,128)(2,1)S(1)}, bf16[4,1,128,768]{2,3,0,1:T(8,128)(2,1)S(1)}, u32[]{:S(2)}, u32[]{:S(2)}) %collective-permute-start.25) | collective-permute-done | bytes 786464 | tf_op jit(solution)/shard_map/ppermute | solution.py:422
  870.0 41.4 %collective-permute-done.41 = bf16[128,2816]{0,1:T(8,128)(2,1)} collective-permute-done((bf16[128,2816]{0,1:T(8,128)(2,1)S(1)}, bf16[128,2816]{0,1:T(8,128)(2,1)}, u32[]{:S(2)}, u32[]{:S(2)}) %collective-permute-start.41) | collective-permute-done | bytes 720928 | tf_op jit(solution)/shard_map/ppermute | solution.py:422
  911.4 12.9 %collective-permute-done.40 = bf16[128,2816]{0,1:T(8,128)(2,1)} collective-permute-done((bf16[128,2816]{0,1:T(8,128)(2,1)S(1)}, bf16[128,2816]{0,1:T(8,128)(2,1)}, u32[]{:S(2)}, u32[]{:S(2)}) %collective-permute-start.40) | collective-permute-done | bytes 720928 | tf_op jit(solution)/shard_map/ppermute | solution.py:422
  (470 shorter events, 349.8 us)
Async XLA Ops:
  7.2 62.9 %all-gather.11.cloned.1.call-start = ((), (), s32[]{:S(2)}) async-start(), calls=%async_computation.2 | async-start | bytes 3833856 | tf_op jit(solution)/shard_map/all_gather | solution.py:493
  35.9 77.4 %all-gather.7.cloned.1.call-start = ((), (), s32[]{:S(2)}) async-start(), calls=%async_computation | async-start | bytes 3833856 | tf_op jit(solution)/shard_map/all_gather | solution.py:493
  36.7 143.5 %all-gather.9.cloned.1.call-start = ((), (), s32[]{:S(2)}) async-start(), calls=%async_computation.1 | async-start | bytes 4325376 | tf_op jit(solution)/shard_map/all_gather | solution.py:496
  37.4 222.8 %all-gather.13.cloned.1.call-start = ((), (), s32[]{:S(2)}) async-start(), calls=%async_computation.3 | async-start | bytes 6488064 | tf_op jit(solution)/shard_map/all_gather | solution.py:496
  38.2 302.2 %all-gather.15.cloned.1.call-start = ((), (), s32[]{:S(2)}) async-start(), calls=%async_computation.4 | async-start | bytes 6488064 | tf_op jit(solution)/shard_map/all_gather | solution.py:496
  39.0 381.5 %all-gather.17.cloned.1.call-start = ((), (), s32[]{:S(2)}) async-start(), calls=%async_computation.5 | async-start | bytes 6488064 | tf_op jit(solution)/shard_map/all_gather | solution.py:496
  112.8 49.9 %collective-permute-start.4 = (bf16[512,512]{1,0:T(8,128)(2,1)S(1)}, bf16[512,512]{1,0:T(8,128)(2,1)S(1)}, u32[]{:S(2)}, u32[]{:S(2)}) collective-permute-start(bf16[512,512]{1,0:T(8,128)(2,1)S(1)} %dynamic-slice_bitcast_fusion), channel_id=1, source_target_pairs={{0,1},{1,0},{2,3},{3,2},{4,5},{5,4},{6,7},{7,6},{8,9},{9,8},{10,11... | collective-permute-start | bytes 1572872 | tf_op jit(solution)/shard_map/ppermute | solution.py:422
  494.7 154.0 %collective-permute-start.35 = (bf16[4,512,512]{2,1,0:T(8,128)(2,1)}, bf16[4,512,512]{2,1,0:T(8,128)(2,1)}, u32[]{:S(2)}, u32[]{:S(2)}) collective-permute-start(bf16[4,512,512]{2,1,0:T(8,128)(2,1)} %pad_maximum_fusion.4), channel_id=1, source_target_pairs={{0,4},{4,0},{8,12},{12,8},{16,20},{20,16},{24,28},{28,24},{1,5},{5... | collective-permute-start | bytes 6291464 | tf_op jit(solution)/shard_map/ppermute | solution.py:422
  625.7 112.1 %collective-permute-start.31 = (bf16[4,512,768]{2,1,0:T(8,128)(2,1)}, bf16[4,512,768]{2,1,0:T(8,128)(2,1)}, u32[]{:S(2)}, u32[]{:S(2)}) collective-permute-start(bf16[4,512,768]{2,1,0:T(8,128)(2,1)} %pad_maximum_fusion.3), channel_id=1, source_target_pairs={{0,4},{4,0},{8,12},{12,8},{16,20},{20,16},{24,28},{28,24},{1,5},{5... | collective-permute-start | bytes 9437192 | tf_op jit(solution)/shard_map/ppermute | solution.py:422
  648.1 108.7 %collective-permute-start.27 = (bf16[4,512,768]{2,1,0:T(8,128)(2,1)}, bf16[4,512,768]{2,1,0:T(8,128)(2,1)}, u32[]{:S(2)}, u32[]{:S(2)}) collective-permute-start(bf16[4,512,768]{2,1,0:T(8,128)(2,1)} %pad_maximum_fusion.2), channel_id=1, source_target_pairs={{0,4},{4,0},{8,12},{12,8},{16,20},{20,16},{24,28},{28,24},{1,5},{5... | collective-permute-start | bytes 9437192 | tf_op jit(solution)/shard_map/ppermute | solution.py:422
  692.3 81.6 %collective-permute-start.23 = (bf16[4,512,768]{2,1,0:T(8,128)(2,1)}, bf16[4,512,768]{2,1,0:T(8,128)(2,1)}, u32[]{:S(2)}, u32[]{:S(2)}) collective-permute-start(bf16[4,512,768]{2,1,0:T(8,128)(2,1)} %pad_maximum_fusion.1), channel_id=1, source_target_pairs={{0,4},{4,0},{8,12},{12,8},{16,20},{20,16},{24,28},{28,24},{1,5},{5... | collective-permute-start | bytes 9437192 | tf_op jit(solution)/shard_map/ppermute | solution.py:422
  753.4 36.4 %collective-permute-start.34 = (bf16[4,1,128,768]{2,3,0,1:T(8,128)(2,1)}, bf16[4,1,128,768]{2,3,0,1:T(8,128)(2,1)}, u32[]{:S(2)}, u32[]{:S(2)}) collective-permute-start(bf16[4,1,128,768]{2,3,0,1:T(8,128)(2,1)} %get-tuple-element.123), channel_id=1, source_target_pairs={{0,24},{4,28},{8,16},{12,20},{16,8},{20,12},{24,0},{28,4},{1,25},{... | collective-permute-start | bytes 2359304 | tf_op jit(solution)/shard_map/ppermute | solution.py:422
  754.8 37.1 %collective-permute-start.33 = (bf16[4,1,128,768]{2,3,0,1:T(8,128)(2,1)S(1)}, bf16[4,1,128,768]{2,3,0,1:T(8,128)(2,1)}, u32[]{:S(2)}, u32[]{:S(2)}) collective-permute-start(bf16[4,1,128,768]{2,3,0,1:T(8,128)(2,1)S(1)} %get-tuple-element.124), channel_id=1, source_target_pairs={{0,16},{4,20},{8,24},{12,28},{16,0},{20,4},{24,8},{28,12},{1,17},{... | collective-permute-start | bytes 2359304 | tf_op jit(solution)/shard_map/ppermute | solution.py:422
  755.8 37.6 %collective-permute-start.32 = (bf16[4,1,128,768]{2,3,0,1:T(8,128)(2,1)S(1)}, bf16[4,1,128,768]{2,3,0,1:T(8,128)(2,1)}, u32[]{:S(2)}, u32[]{:S(2)}) collective-permute-start(bf16[4,1,128,768]{2,3,0,1:T(8,128)(2,1)S(1)} %get-tuple-element.122), channel_id=1, source_target_pairs={{0,8},{4,12},{8,0},{12,4},{16,24},{20,28},{24,16},{28,20},{1,9},{5... | collective-permute-start | bytes 2359304 | tf_op jit(solution)/shard_map/ppermute | solution.py:422
  773.9 51.8 %collective-permute-start.29 = (bf16[4,1,128,768]{2,3,0,1:T(8,128)(2,1)S(1)}, bf16[4,1,128,768]{2,3,0,1:T(8,128)(2,1)}, u32[]{:S(2)}, u32[]{:S(2)}) collective-permute-start(bf16[4,1,128,768]{2,3,0,1:T(8,128)(2,1)S(1)} %get-tuple-element.121), channel_id=1, source_target_pairs={{0,16},{4,20},{8,24},{12,28},{16,0},{20,4},{24,8},{28,12},{1,17},{... | collective-permute-start | bytes 2359304 | tf_op jit(solution)/shard_map/ppermute | solution.py:422
  789.8 38.7 %collective-permute-start.28 = (bf16[4,1,128,768]{2,3,0,1:T(8,128)(2,1)S(1)}, bf16[4,1,128,768]{2,3,0,1:T(8,128)(2,1)S(1)}, u32[]{:S(2)}, u32[]{:S(2)}) collective-permute-start(bf16[4,1,128,768]{2,3,0,1:T(8,128)(2,1)S(1)} %get-tuple-element.119), channel_id=1, source_target_pairs={{0,8},{4,12},{8,0},{12,4},{16,24},{20,28},{24,16},{28,20},{1,9},{5... | collective-permute-start | bytes 2359304 | tf_op jit(solution)/shard_map/ppermute | solution.py:422
  791.9 50.5 %collective-permute-start.26 = (bf16[4,1,128,768]{2,3,0,1:T(8,128)(2,1)S(1)}, bf16[4,1,128,768]{2,3,0,1:T(8,128)(2,1)S(1)}, u32[]{:S(2)}, u32[]{:S(2)}) collective-permute-start(bf16[4,1,128,768]{2,3,0,1:T(8,128)(2,1)S(1)} %get-tuple-element.117), channel_id=1, source_target_pairs={{0,24},{4,28},{8,16},{12,20},{16,8},{20,12},{24,0},{28,4},{1,25},{... | collective-permute-start | bytes 2359304 | tf_op jit(solution)/shard_map/ppermute | solution.py:422
  793.3 63.1 %collective-permute-start.25 = (bf16[4,1,128,768]{2,3,0,1:T(8,128)(2,1)S(1)}, bf16[4,1,128,768]{2,3,0,1:T(8,128)(2,1)S(1)}, u32[]{:S(2)}, u32[]{:S(2)}) collective-permute-start(bf16[4,1,128,768]{2,3,0,1:T(8,128)(2,1)S(1)} %get-tuple-element.118), channel_id=1, source_target_pairs={{0,16},{4,20},{8,24},{12,28},{16,0},{20,4},{24,8},{28,12},{1,17},{... | collective-permute-start | bytes 2359304 | tf_op jit(solution)/shard_map/ppermute | solution.py:422
  808.7 47.7 %collective-permute-start.24 = (bf16[4,1,128,768]{2,3,0,1:T(8,128)(2,1)S(1)}, bf16[4,1,128,768]{2,3,0,1:T(8,128)(2,1)S(1)}, u32[]{:S(2)}, u32[]{:S(2)}) collective-permute-start(bf16[4,1,128,768]{2,3,0,1:T(8,128)(2,1)S(1)} %get-tuple-element.116), channel_id=1, source_target_pairs={{0,8},{4,12},{8,0},{12,4},{16,24},{20,28},{24,16},{28,20},{1,9},{5... | collective-permute-start | bytes 2359304 | tf_op jit(solution)/shard_map/ppermute | solution.py:422
  825.6 40.4 %collective-permute-start.22 = (bf16[128,1664]{0,1:T(8,128)(2,1)S(1)}, bf16[128,1664]{0,1:T(8,128)(2,1)S(1)}, u32[]{:S(2)}, u32[]{:S(2)}) collective-permute-start(bf16[128,1664]{0,1:T(8,128)(2,1)S(1)} %select_convert_fusion), channel_id=1, source_target_pairs={{2,1},{1,2},{6,5},{5,6},{10,9},{9,10},{14,13},{13,14},{18,17},{17,... | collective-permute-start | bytes 1277960 | tf_op jit(solution)/shard_map/ppermute | solution.py:609
  828.5 37.5 %collective-permute-start.21 = (bf16[128,1664]{0,1:T(8,128)(2,1)S(1)}, bf16[128,1664]{0,1:T(8,128)(2,1)S(1)}, u32[]{:S(2)}, u32[]{:S(2)}) collective-permute-start(bf16[128,1664]{0,1:T(8,128)(2,1)S(1)} %copy-done.51), channel_id=1, source_target_pairs={{0,1},{1,3},{3,2},{2,0},{4,5},{5,7},{7,6},{6,4},{8,9},{9,11},{11,1... | collective-permute-start | bytes 1277960 | tf_op jit(solution)/shard_map/ppermute | solution.py:607
  861.4 50.1 %collective-permute-start.41 = (bf16[128,2816]{0,1:T(8,128)(2,1)S(1)}, bf16[128,2816]{0,1:T(8,128)(2,1)}, u32[]{:S(2)}, u32[]{:S(2)}) collective-permute-start(bf16[128,2816]{0,1:T(8,128)(2,1)S(1)} %get-tuple-element.114), channel_id=1, source_target_pairs={{0,3},{1,2},{2,1},{3,0},{4,7},{5,6},{6,5},{7,4},{8,11},{9,10},{10,... | collective-permute-start | bytes 2162696 | tf_op jit(solution)/shard_map/ppermute | solution.py:422
  862.4 61.9 %collective-permute-start.40 = (bf16[128,2816]{0,1:T(8,128)(2,1)S(1)}, bf16[128,2816]{0,1:T(8,128)(2,1)}, u32[]{:S(2)}, u32[]{:S(2)}) collective-permute-start(bf16[128,2816]{0,1:T(8,128)(2,1)S(1)} %get-tuple-element.115), channel_id=1, source_target_pairs={{0,2},{1,3},{2,0},{3,1},{4,6},{5,7},{6,4},{7,5},{8,10},{9,11},{10,... | collective-permute-start | bytes 2162696 | tf_op jit(solution)/shard_map/ppermute | solution.py:422
  866.0 58.3 %collective-permute-start.39 = (bf16[128,2816]{0,1:T(8,128)(2,1)S(1)}, bf16[128,2816]{0,1:T(8,128)(2,1)}, u32[]{:S(2)}, u32[]{:S(2)}) collective-permute-start(bf16[128,2816]{0,1:T(8,128)(2,1)S(1)} %get-tuple-element.113), channel_id=1, source_target_pairs={{0,1},{1,0},{2,3},{3,2},{4,5},{5,4},{6,7},{7,6},{8,9},{9,8},{10,11... | collective-permute-start | bytes 2162696 | tf_op jit(solution)/shard_map/ppermute | solution.py:422
  (115 other events, 1232.3 us)
Sparse Core Ops, SparseCore 0:
  36.0 34.0 all-gather.10
  72.0 33.8 all-gather.6
  108.7 71.3 all-gather.8
  183.5 76.6 all-gather.12
  263.5 76.8 all-gather.14
  343.6 76.8 all-gather.16

commit v3 on v2

--- a/solution.py
+++ b/solution.py
@@ -5,6 +5,7 @@
 from jax.experimental import pallas as pl
 from jax.experimental.pallas import tpu as pltpu
 from jax.sharding import PartitionSpec as P
+
 
 DK = 128
 DV = 256
@@ -100,7 +101,7 @@
     return found
 
 
-def gather_inputs(first, start, end, refs, heads, block):
+def gather_inputs(first, start, end, refs, block):
     pre_q, pre_k, pre_v, pre_ab, halo_q, halo_k, halo_v, taps_q, taps_k, taps_v, rate, bias = refs
     valid = valid_rows(first, block, start, end)
     halo_valid = valid_rows(first - 8, 8, start, end)
@@ -152,7 +153,7 @@
         state[...] = jnp.zeros_like(state)
 
     refs = (pre_q, pre_k, pre_v, pre_ab, halo_q, halo_k, halo_v, taps_q, taps_k, taps_v, rate, bias)
-    common = gather_inputs(step * block, bounds[0, row], bounds[1, row], refs, heads, block)
+    common = gather_inputs(step * block, bounds[0, row], bounds[1, row], refs, block)
     ops = [head_operands(common, head, heads, block) for head in range(heads)]
     at, to = triangle(block)
     systems = [jnp.where(at > to, o["beta"] * o["spread"] * mm(o["k"], o["k"], 1, 1), 0.0) for o in ops]
@@ -199,7 +200,7 @@
             ref[...] = jnp.zeros_like(ref)
 
     refs = (pre_q, pre_k, pre_v, pre_ab, halo_q, halo_k, halo_v, taps_q, taps_k, taps_v, rate, bias)
-    common = gather_inputs(step * block, bounds[0, row], bounds[1, row], refs, heads, block)
+    common = gather_inputs(step * block, bounds[0, row], bounds[1, row], refs, block)
     valid = common["valid"]
     at, to = triangle(block)
     lane = lax.broadcasted_iota(jnp.int32, (block, LANES), 1)
@@ -434,27 +435,39 @@
     return (jnp.arange(width, dtype=jnp.int32)[:, None] == source[None, :]).astype(BF16)
 
 
-def scatter_sum(product, left, devices):
+def scatter_sum(left, right, devices):
     half = left.shape[1] // 2
     block = half * 2 // devices
-    got = swap(product(left[:, half:]).astype(BF16), "dp", devices, 1)
-    keep = product(left[:, :half]) + got.astype(F32)
+    got = swap(inner(left[:, half:], right).astype(BF16), "dp", devices, 1)
+    keep = inner(left[:, :half], right) + got.astype(F32)
     count, stride = devices // 2, 2
-    lead = keep.shape[:-2]
     while count > 1:
         ways = min(4, count)
-        shaped = keep.reshape(lead + (count // ways, ways, block, keep.shape[-1]))
-        keep = shaped[..., :, 0, :, :]
+        shaped = keep.reshape(count // ways, ways, block, keep.shape[-1])
+        keep = shaped[:, 0]
         for way in range(1, ways):
-            sent = shaped[..., :, way, :, :].astype(BF16)
-            keep = keep + swap(sent, "dp", devices, way * stride).astype(F32)
+            got = swap(shaped[:, way].astype(BF16), "dp", devices, way * stride)
+            keep = keep + got.astype(F32)
         count //= ways
         stride *= ways
-        keep = keep.reshape(lead + (count * block, keep.shape[-1]))
+        keep = keep.reshape(count * block, keep.shape[-1])
     return keep
 
 
-def shards(
+def gather_relative(value, devices):
+    count, stride = devices // 2, 2
+    while count > 1:
+        ways = min(4, count)
+        parts = [value]
+        for way in range(1, ways):
+            parts.append(swap(value, "dp", devices, way * stride))
+        value = jnp.concatenate(parts, 0)
+        count //= ways
+        stride *= ways
+    return value, swap(value, "dp", devices, 1)
+
+
+def compute(
     tokens, lengths, starts, norm_one, w_query, w_key, w_value, w_gating, w_decay, w_strength,
     filter_query, filter_key, filter_value, decay_log, decay_bias, head_gain, w_output, norm_two,
     w_gate, w_up, w_down, cotangent,
@@ -482,7 +495,13 @@
     inputs = tokens.astype(F32)
     scale_one = lax.rsqrt(jnp.mean(inputs * inputs, -1, keepdims=True) + 1e-05)
     normed_one = (inputs * scale_one * norm_one).astype(BF16)
-    row_one = both_halves(normed_one, exchange(normed_one))
+    relative = relative_matrix(width, devices, me)
+
+    def to_relative(value):
+        return matmul(value, relative).astype(BF16)
+
+    one_local = to_relative(normed_one)
+    one_rel = both_halves(one_local, exchange(one_local))
 
     spare = jnp.zeros((w_query.shape[0], LANES - 2 * HEADS), BF16)
     packed = jnp.concatenate([w_query, w_key, w_value, w_gating, w_decay, w_strength, spare], 1)
@@ -490,7 +509,7 @@
     second = lax.ppermute(packed, "tensor", [(1, 2), (2, 1)])
     lower = jnp.where(rank == 0, packed, jnp.where(rank == 1, second, first))
     upper = jnp.where(rank == 3, packed, jnp.where(rank == 2, second, first))
-    mixer_weights = [lax.all_gather(w, "dp", axis=0, tiled=True) for w in (lower, upper)]
+    mixer_weights = [gather_relative(w, devices) for w in (lower, upper)]
 
     def gather(value):
         whole = lax.all_gather(value, ("tensor", "dp"), axis=0, tiled=True)
@@ -517,7 +536,8 @@
 
     shard_ids = [2 * half, 2 * half + 1]
     smalls = [small_of(s) for s in shard_ids]
-    pres = [matmul(row_one, w)[None] for w in mixer_weights]
+    near, far = one_rel[:, : width // 2], one_rel[:, width // 2 :]
+    pres = [(matmul(near, w[0]) + matmul(far, w[1]))[None] for w in mixer_weights]
     saves, own, got = [], [], []
     for pre, small in zip(pres, smalls):
         mixed, *saved = mixer_forward(bounds, pre, small)
@@ -531,11 +551,6 @@
     middle = inputs + attention
     scale_two = lax.rsqrt(jnp.mean(middle * middle, -1, keepdims=True) + 1e-05)
     normed_two = (middle * scale_two * norm_two).astype(BF16)
-
-    relative = relative_matrix(width, devices, me)
-
-    def to_relative(value):
-        return matmul(value, relative).astype(BF16)
 
     residual_grad = cotangent.astype(F32) * mask
     feed_grad = residual_grad.astype(BF16)
@@ -561,12 +576,12 @@
         two_grad = part if two_grad is None else two_grad + part
     block_out = (mask * (middle + feed)).astype(BF16)
 
-    def many(values):
-        return lambda left: jnp.stack([inner(left, v) for v in values])
-
-    sum_gate = scatter_sum(many(gate_grads), two_rel, devices)
-    sum_up = scatter_sum(many(up_grads), two_rel, devices)
-    sum_down = scatter_sum(many(hiddens), feed_rel, devices)
+    def wide_sum(left, values):
+        return scatter_sum(left, jnp.concatenate(values, 1), devices)
+
+    sum_gate = wide_sum(two_rel, gate_grads)
+    sum_up = wide_sum(two_rel, up_grads)
+    sum_down = wide_sum(feed_rel, hiddens)
 
     middle_part, grad_norm_two = norm_backward(two_grad, middle, scale_two, norm_two)
     middle_grad = residual_grad + middle_part
@@ -576,25 +591,33 @@
         sent = matmul(attention_grad, out_t[2 * (1 - half) + j]).astype(BF16)
         kept = matmul(attention_grad, out_t[2 * half + j]).astype(BF16)
         mixed_grads.append(both_halves(kept, exchange(sent))[None])
-    sum_out = scatter_sum(many(mixed), to_relative(attention_grad), devices)
-
-    one_rel = to_relative(row_one)
+    sum_out = wide_sum(to_relative(attention_grad), mixed)
+
     one_part = None
     mixer_sums, smalls_grads = [], []
     for j in range(2):
         d_pre, *d_small = mixer_backward(bounds, pres[j], smalls[j], saves[j], mixed_grads[j])
         d_pre = d_pre[0]
         smalls_grads.append(d_small)
-        mixer_sums.append(scatter_sum(lambda left: inner(left, d_pre), one_rel, devices))
-        part = matmul_t(d_pre, mixer_weights[j])
-        one_part = part if one_part is None else one_part + part
+        mixer_sums.append(scatter_sum(one_rel, d_pre, devices))
+        part = [matmul_t(d_pre, w) for w in mixer_weights[j]]
+        one_part = part if one_part is None else [a + b for a, b in zip(one_part, part)]
+    one_part = jnp.concatenate(one_part, 1)
     one_kept = lax.dynamic_slice_in_dim(one_part, half * tok_dev, tok_dev)
     one_sent = lax.dynamic_slice_in_dim(one_part, (1 - half) * tok_dev, tok_dev)
     one_grad = one_kept + exchange(one_sent.astype(BF16)).astype(F32)
+    one_grad = sum(matmul_t(piece, relative) for piece in halves(one_grad))
     input_part, grad_norm_one = norm_backward(one_grad, inputs, scale_one, norm_one)
     grad_tokens = middle_grad + input_part
 
-    feeds = jnp.concatenate([sum_gate, sum_up, sum_down, sum_out], -1)
+    def shard_part(value, t):
+        size = value.shape[1] // ranks
+        return value[:, t * size : (t + 1) * size]
+
+    feeds = jnp.stack([
+        jnp.concatenate([shard_part(v, t) for v in (sum_gate, sum_up, sum_down, sum_out)], 1)
+        for t in range(ranks)
+    ])
     owned = feeds[rank]
     for mask_z in range(1, ranks):
         owned = owned + swap(feeds[rank ^ mask_z].astype(BF16), "tensor", ranks, mask_z).astype(F32)
@@ -681,7 +704,7 @@
         P(("dp", "tensor"), None),
     )
     return jax.shard_map(
-        shards,
+        compute,
         mesh=mesh,
         in_specs=placed,
         out_specs=(

time: 947 us -> 860 us (0.908)
  waiting for transfers between devices: 426 us -> 333 us
  other arithmetic: 67.9 us -> 49.5 us
  local copies, waits for them, and re-layouts: 80.3 us -> 90.4 us
    all_gather x4, waiting for transfers between devices: 199 us -> 103 us  [gather(): whole = lax.all_gather(value, ('tensor', 'dp'), axis=0, tiled=True)]
    add x14 -> x10, other arithmetic: 23 us -> 6.35 us  [the longest x1 2.3 us: compute(): owned + swap(feeds[rank ^ mask_z].astype(BF16), 'tensor', ranks, mask_z)....]
    unnamed x194 -> x272, local copies, waits for them, and re-layouts: 13.4 us -> 20.8 us
    another operation x11 -> x12, other arithmetic: 22.7 us -> 15.5 us
    ppermute x38 -> x46, waiting for transfers between devices: 201 us -> 208 us  [swap(): return lax.ppermute(value, axis, [(i, i ^ mask) for i in range(size)])]
    ppermute x38 -> x46, starting transfers between devices: 38.1 us -> 44.6 us  [swap(): return lax.ppermute(value, axis, [(i, i ^ mask) for i in range(size)])]
    dot_general x18 -> x22, matrix products: 39.2 us -> 44.2 us  [matmul_t(): lax.dot_general(left, right, (((1,), (1,)), ((), ())), preferred_element_...]
    dot_general x22 -> x24, matrix products: 68 us -> 70.6 us  [matmul(): return jnp.dot(left, right, preferred_element_type=F32)]
  transfers between devices with their start and end apart: 48 -> 54, of which waited for: 24 -> 24; matrix products, arithmetic and copies ran while one was open for 25% -> 31% of each run, Pallas kernels for 15% -> 16%
where the time goes in v3:
time: 860 us; the launch traced here: 848 us
  waiting for transfers between devices  333 us (39%)
  matrix products  172 us (20%)
  Pallas kernels  136 us (16%)
  local copies, waits for them, and re-layouts  90.4 us (11%)
  starting transfers between devices  51.3 us (6%)
  other arithmetic  49.5 us (6%)
  between operations  15.9 us (2%)
    ppermute x46, waiting for transfers between devices, swap(): return lax.ppermute(value, axis, [(i, i ^ mask) for i in range(size)])  208 us
    all_gather x4, waiting for transfers between devices, gather(): whole = lax.all_gather(value, ('tensor', 'dp'), axis=0, tiled=True)  103 us
    pallas_call x2, Pallas kernels, mixer_backward(): pl.pallas_call(functools.partial(backward_kernel, HEADS, BLOCK, steps), g...  72 us
    dot_general x24, matrix products, matmul(): return jnp.dot(left, right, preferred_element_type=F32)  70.6 us
    pallas_call x2, Pallas kernels, mixer_forward(): pl.pallas_call(functools.partial(forward_kernel, HEADS, BLOCK), grid_spec...  63.9 us
    dot_general x12, matrix products, inner(): lax.dot_general(left, right, (((0,), (0,)), ((), ())), preferred_element_...  57.4 us
    ppermute x46, starting transfers between devices, swap(): return lax.ppermute(value, axis, [(i, i ^ mask) for i in range(size)])  44.6 us
    dot_general x22, matrix products, matmul_t(): lax.dot_general(left, right, (((1,), (1,)), ((), ())), preferred_element_...  44.2 us
  transfers between devices with their start and end apart: 54, of which 24 were waited for; matrix products, arithmetic and copies ran while one was open for 31% of the time, Pallas kernels for 16%

profile of v3, /device:TPU:8, one launch (start us, length us, event | category | flops | bytes accessed | tf_op | source)
XLA Modules:
  0.0 848.1 jit_solution(3177208185020658451)
XLA Ops:
  20.5 21.7 %collective-permute-done.1 = bf16[128,1664]{0,1:T(8,128)(2,1)S(1)} collective-permute-done((bf16[128,1664]{0,1:T(8,128)(2,1)S(1)}, bf16[128,1664]{0,1:T(8,128)(2,1)S(1)}, u32[]{:S(2)}, u32[]{:S(2)}) %collective-permute-start.1) | collective-permute-done | bytes 426016 | tf_op jit(solution)/shard_map/ppermute | solution.py:509
  49.5 7.5 collective-permute-done.10
  57.0 6.1 collective-permute-done.9
  75.9 13.8 %collective-permute-done.5 = bf16[128,1664]{0,1:T(8,128)(2,1)S(1)} collective-permute-done((bf16[128,1664]{0,1:T(8,128)(2,1)S(1)}, bf16[128,1664]{0,1:T(8,128)(2,1)S(1)}, u32[]{:S(2)}, u32[]{:S(2)}) %collective-permute-start.5) | collective-permute-done | bytes 426016 | tf_op jit(solution)/shard_map/ppermute | solution.py:423
  113.1 32.0 %mixer_forward.3 = (bf16[1,1024,512]{2,1,0:T(8,128)(2,1)}, f32[1,1024,512]{2,1,0:T(8,128)}, f32[1,4,2,128,256]{4,3,2,1,0:T(8,128)}, f32[1,1024,512]{2,1,0:T(8,128)}, f32[1,4,2,256,256]{4,3,2,1,0:T(8,128)}) custom-call(s32[2,1]{1,0:T(2,128)} %constant_dynamic-slice_fusion.6.bounds, ...), custom_call_target="tpu_custom_call" | custom-call | flops 10000000000 | bytes 20000000 | tf_op jit(solution)/shard_map/mixer_forward/pallas_call | solution.py:330
  155.8 32.0 %mixer_forward.2 = (bf16[1,1024,512]{2,1,0:T(8,128)(2,1)}, f32[1,1024,512]{2,1,0:T(8,128)}, f32[1,4,2,128,256]{4,3,2,1,0:T(8,128)}, f32[1,1024,512]{2,1,0:T(8,128)}, f32[1,4,2,256,256]{4,3,2,1,0:T(8,128)}) custom-call(s32[2,1]{1,0:T(2,128)} %constant_dynamic-slice_fusion.6.bounds, ...), custom_call_target="tpu_custom_call" | custom-call | flops 10000000000 | bytes 20000000 | tf_op jit(solution)/shard_map/mixer_forward/pallas_call | solution.py:330
  196.6 6.6 collective-permute-done.7
  203.5 7.2 copy.67
  228.0 41.9 %all-gather.9.cloned.1.call-done = bf16[4096,768]{0,1:T(8,128)(2,1)} async-done(((bf16[128,768]{0,1:T(8,128)(2,1)}), bf16[4096,768]{0,1:T(8,128)(2,1)}) %all-gather.9.cloned.1.call-update) | async-done | bytes 6291472 | tf_op jit(solution)/shard_map/all_gather | solution.py:515
  289.4 60.6 %all-gather.11.cloned.1.call-done = bf16[4096,768]{0,1:T(8,128)(2,1)} async-done(((bf16[128,768]{0,1:T(8,128)(2,1)}), bf16[4096,768]{0,1:T(8,128)(2,1)}) %all-gather.11.cloned.1.call-update) | async-done | bytes 6291472 | tf_op jit(solution)/shard_map/all_gather | solution.py:515
  412.6 35.9 %mixer_backward.3 = (bf16[1,1024,1664]{2,1,0:T(8,128)(2,1)}, f32[8,256]{1,0:T(8,128)}, f32[8,256]{1,0:T(8,128)}, f32[8,512]{1,0:T(8,128)}, f32[8,128]{1,0:T(8,128)}, /*index=5*/f32[8,256]{1,0:T(8,128)}) custom-call(s32[2,1]{1,0:T(2,128)} %constant_dynamic-slice_fusion.6.bounds, ...), custom_call_target="tpu_custom_call" | custom-call | flops 10000000000 | bytes 20000000 | tf_op jit(solution)/shard_map/mixer_backward/pallas_call | solution.py:367
  448.5 36.1 %mixer_backward.2 = (bf16[1,1024,1664]{2,1,0:T(8,128)(2,1)}, f32[8,256]{1,0:T(8,128)}, f32[8,256]{1,0:T(8,128)}, f32[8,512]{1,0:T(8,128)}, f32[8,128]{1,0:T(8,128)}, /*index=5*/f32[8,256]{1,0:T(8,128)}) custom-call(s32[2,1]{1,0:T(2,128)} %constant_dynamic-slice_fusion.6.bounds, ...), custom_call_target="tpu_custom_call" | custom-call | flops 10000000000 | bytes 20000000 | tf_op jit(solution)/shard_map/mixer_backward/pallas_call | solution.py:367
  504.1 19.4 %collective-permute-done.15 = bf16[512,1024]{0,1:T(8,128)(2,1)S(1)} collective-permute-done((bf16[512,1024]{0,1:T(8,128)(2,1)S(1)}, bf16[512,1024]{0,1:T(8,128)(2,1)S(1)}, u32[]{:S(2)}, u32[]{:S(2)}) %collective-permute-start.15) | collective-permute-done | bytes 1048608 | tf_op jit(solution)/shard_map/ppermute | solution.py:423
  611.1 7.8 collective-permute-done.23
  641.7 6.1 convert_add_fusion
  647.8 6.6 copy.76
  667.1 6.6 copy.74
  685.4 6.5 copy.72
  702.1 15.4 %collective-permute-done.38 = bf16[1,128,3072]{1,2,0:T(8,128)(2,1)S(1)} collective-permute-done((bf16[1,128,3072]{1,2,0:T(8,128)(2,1)S(1)}, bf16[1,128,3072]{1,2,0:T(8,128)(2,1)S(1)}, u32[]{:S(2)}, u32[]{:S(2)}) %collective-permute-start.38) | collective-permute-done | bytes 786464 | tf_op jit(solution)/shard_map/ppermute | solution.py:423
  718.7 15.1 %collective-permute-done.37 = bf16[1,128,3072]{1,2,0:T(8,128)(2,1)S(1)} collective-permute-done((bf16[1,128,3072]{1,2,0:T(8,128)(2,1)S(1)}, bf16[1,128,3072]{1,2,0:T(8,128)(2,1)S(1)}, u32[]{:S(2)}, u32[]{:S(2)}) %collective-permute-start.37) | collective-permute-done | bytes 786464 | tf_op jit(solution)/shard_map/ppermute | solution.py:423
  737.9 13.3 %collective-permute-done.34 = bf16[1,128,3072]{1,2,0:T(8,128)(2,1)S(1)} collective-permute-done((bf16[1,128,3072]{1,2,0:T(8,128)(2,1)S(1)}, bf16[1,128,3072]{1,2,0:T(8,128)(2,1)S(1)}, u32[]{:S(2)}, u32[]{:S(2)}) %collective-permute-start.34) | collective-permute-done | bytes 786464 | tf_op jit(solution)/shard_map/ppermute | solution.py:423
  751.3 14.8 %collective-permute-done.33 = bf16[1,128,3072]{1,2,0:T(8,128)(2,1)S(1)} collective-permute-done((bf16[1,128,3072]{1,2,0:T(8,128)(2,1)S(1)}, bf16[1,128,3072]{1,2,0:T(8,128)(2,1)S(1)}, u32[]{:S(2)}, u32[]{:S(2)}) %collective-permute-start.33) | collective-permute-done | bytes 786464 | tf_op jit(solution)/shard_map/ppermute | solution.py:423
  782.6 40.8 %collective-permute-done.49 = bf16[128,2816]{0,1:T(8,128)(2,1)} collective-permute-done((bf16[128,2816]{0,1:T(8,128)(2,1)S(1)}, bf16[128,2816]{0,1:T(8,128)(2,1)}, u32[]{:S(2)}, u32[]{:S(2)}) %collective-permute-start.49) | collective-permute-done | bytes 720928 | tf_op jit(solution)/shard_map/ppermute | solution.py:423
  823.4 13.9 %collective-permute-done.48 = bf16[128,2816]{0,1:T(8,128)(2,1)} collective-permute-done((bf16[128,2816]{0,1:T(8,128)(2,1)S(1)}, bf16[128,2816]{0,1:T(8,128)(2,1)}, u32[]{:S(2)}, u32[]{:S(2)}) %collective-permute-start.48) | collective-permute-done | bytes 720928 | tf_op jit(solution)/shard_map/ppermute | solution.py:423
  (541 shorter events, 364.4 us)
Async XLA Ops:
  7.2 196.2 %all-gather.5.cloned.1.call-start = ((), (), s32[]{:S(2)}) async-start(), calls=%async_computation | async-start | bytes 4325376 | tf_op jit(solution)/shard_map/all_gather | solution.py:515
  8.0 212.4 %all-gather.7.cloned.1.call-start = ((), (), s32[]{:S(2)}) async-start(), calls=%async_computation.1 | async-start | bytes 6488064 | tf_op jit(solution)/shard_map/all_gather | solution.py:515
  9.7 260.3 %all-gather.9.cloned.1.call-start = ((), (), s32[]{:S(2)}) async-start(), calls=%async_computation.2 | async-start | bytes 6488064 | tf_op jit(solution)/shard_map/all_gather | solution.py:515
  11.3 338.7 %all-gather.11.cloned.1.call-start = ((), (), s32[]{:S(2)}) async-start(), calls=%async_computation.3 | async-start | bytes 6488064 | tf_op jit(solution)/shard_map/all_gather | solution.py:515
  49.3 50.0 %collective-permute-start = (bf16[512,1024]{1,0:T(8,128)(2,1)}, bf16[512,1024]{1,0:T(8,128)(2,1)}, u32[]{:S(2)}, u32[]{:S(2)}) collective-permute-start(bf16[512,1024]{1,0:T(8,128)(2,1)} %fusion.73), channel_id=1, source_target_pairs={{0,1},{1,0},{2,3},{3,2},{4,5},{5,4},{6,7},{7,6},{8,9},{9,8},{10,11... | collective-permute-start | bytes 3145736 | tf_op jit(solution)/shard_map/ppermute | solution.py:423
  65.7 37.0 %collective-permute-start.11 = (bf16[512,1664]{0,1:T(8,128)(2,1)}, bf16[512,1664]{0,1:T(8,128)(2,1)}, u32[]{:S(2)}, u32[]{:S(2)}) collective-permute-start(bf16[512,1664]{0,1:T(8,128)(2,1)} %pad_maximum_fusion.6), channel_id=1, source_target_pairs={{0,4},{4,0},{8,12},{12,8},{16,20},{20,16},{24,28},{28,24},{1,5},{5... | collective-permute-start | bytes 5111816 | tf_op jit(solution)/shard_map/ppermute | solution.py:423
  99.2 47.8 %collective-permute-start.6 = (bf16[512,1664]{0,1:T(8,128)(2,1)}, bf16[512,1664]{0,1:T(8,128)(2,1)}, u32[]{:S(2)}, u32[]{:S(2)}) collective-permute-start(bf16[512,1664]{0,1:T(8,128)(2,1)} %pad_maximum_fusion.5), channel_id=1, source_target_pairs={{0,4},{4,0},{8,12},{12,8},{16,20},{20,16},{24,28},{28,24},{1,5},{5... | collective-permute-start | bytes 5111816 | tf_op jit(solution)/shard_map/ppermute | solution.py:423
  146.9 47.5 %collective-permute-start.12 = (bf16[512,512]{1,0:T(8,128)(2,1)}, bf16[512,512]{1,0:T(8,128)(2,1)}, u32[]{:S(2)}, u32[]{:S(2)}) collective-permute-start(bf16[512,512]{1,0:T(8,128)(2,1)} %dynamic-slice_bitcast_fusion), channel_id=1, source_target_pairs={{0,1},{1,0},{2,3},{3,2},{4,5},{5,4},{6,7},{7,6},{8,9},{9,8},{10,11... | collective-permute-start | bytes 1572872 | tf_op jit(solution)/shard_map/ppermute | solution.py:423
  393.2 165.1 %collective-permute-start.43 = (bf16[512,2048]{1,0:T(8,128)(2,1)}, bf16[512,2048]{1,0:T(8,128)(2,1)}, u32[]{:S(2)}, u32[]{:S(2)}) collective-permute-start(bf16[512,2048]{1,0:T(8,128)(2,1)} %convolution_convert_fusion.3), channel_id=1, source_target_pairs={{0,4},{4,0},{8,12},{12,8},{16,20},{20,16},{24,28},{28,24},{1,5},{5... | collective-permute-start | bytes 6291464 | tf_op jit(solution)/shard_map/ppermute | solution.py:423
  534.0 107.6 %collective-permute-start.39 = (bf16[512,3072]{1,0:T(8,128)(2,1)}, bf16[512,3072]{1,0:T(8,128)(2,1)}, u32[]{:S(2)}, u32[]{:S(2)}) collective-permute-start(bf16[512,3072]{1,0:T(8,128)(2,1)} %convolution_convert_fusion), channel_id=1, source_target_pairs={{0,4},{4,0},{8,12},{12,8},{16,20},{20,16},{24,28},{28,24},{1,5},{5... | collective-permute-start | bytes 9437192 | tf_op jit(solution)/shard_map/ppermute | solution.py:423
  544.2 46.4 %collective-permute-start.25 = (bf16[512,1664]{1,0:T(8,128)(2,1)}, bf16[512,1664]{1,0:T(8,128)(2,1)}, u32[]{:S(2)}, u32[]{:S(2)}) collective-permute-start(bf16[512,1664]{1,0:T(8,128)(2,1)} %fusion.30), channel_id=1, source_target_pairs={{0,4},{4,0},{8,12},{12,8},{16,20},{20,16},{24,28},{28,24},{1,5},{5... | collective-permute-start | bytes 5111816 | tf_op jit(solution)/shard_map/ppermute | solution.py:423
  604.1 55.6 %collective-permute-start.35 = (bf16[512,3072]{1,0:T(8,128)(2,1)}, bf16[512,3072]{1,0:T(8,128)(2,1)}, u32[]{:S(2)}, u32[]{:S(2)}) collective-permute-start(bf16[512,3072]{1,0:T(8,128)(2,1)} %convolution_convert_fusion.1), channel_id=1, source_target_pairs={{0,4},{4,0},{8,12},{12,8},{16,20},{20,16},{24,28},{28,24},{1,5},{5... | collective-permute-start | bytes 9437192 | tf_op jit(solution)/shard_map/ppermute | solution.py:423
  628.3 49.7 %collective-permute-start.31 = (bf16[512,3072]{1,0:T(8,128)(2,1)}, bf16[512,3072]{1,0:T(8,128)(2,1)}, u32[]{:S(2)}, u32[]{:S(2)}) collective-permute-start(bf16[512,3072]{1,0:T(8,128)(2,1)} %convolution_convert_fusion.2), channel_id=1, source_target_pairs={{0,4},{4,0},{8,12},{12,8},{16,20},{20,16},{24,28},{28,24},{1,5},{5... | collective-permute-start | bytes 9437192 | tf_op jit(solution)/shard_map/ppermute | solution.py:423
  638.6 138.8 %collective-permute-start.30 = (bf16[128,1664]{0,1:T(8,128)(2,1)}, bf16[128,1664]{0,1:T(8,128)(2,1)}, u32[]{:S(2)}, u32[]{:S(2)}) collective-permute-start(bf16[128,1664]{0,1:T(8,128)(2,1)} %select_convert_fusion), channel_id=1, source_target_pairs={{2,1},{1,2},{6,5},{5,6},{10,9},{9,10},{14,13},{13,14},{18,17},{17,... | collective-permute-start | bytes 1277960 | tf_op jit(solution)/shard_map/ppermute | solution.py:632
  641.5 135.8 %collective-permute-start.29 = (bf16[128,1664]{0,1:T(8,128)(2,1)}, bf16[128,1664]{0,1:T(8,128)(2,1)}, u32[]{:S(2)}, u32[]{:S(2)}) collective-permute-start(bf16[128,1664]{0,1:T(8,128)(2,1)} %get-tuple-element.108), channel_id=1, source_target_pairs={{0,1},{1,3},{3,2},{2,0},{4,5},{5,7},{7,6},{6,4},{8,9},{9,11},{11,1... | collective-permute-start | bytes 1277960 | tf_op jit(solution)/shard_map/ppermute | solution.py:630
  658.6 36.6 %collective-permute-start.42 = (bf16[1,128,3072]{1,2,0:T(8,128)(2,1)}, bf16[1,128,3072]{1,2,0:T(8,128)(2,1)}, u32[]{:S(2)}, u32[]{:S(2)}) collective-permute-start(bf16[1,128,3072]{1,2,0:T(8,128)(2,1)} %get-tuple-element.123), channel_id=1, source_target_pairs={{0,24},{4,28},{8,16},{12,20},{16,8},{20,12},{24,0},{28,4},{1,25},{... | collective-permute-start | bytes 2359304 | tf_op jit(solution)/shard_map/ppermute | solution.py:423
  659.6 37.7 %collective-permute-start.41 = (bf16[1,128,3072]{1,2,0:T(8,128)(2,1)S(1)}, bf16[1,128,3072]{1,2,0:T(8,128)(2,1)}, u32[]{:S(2)}, u32[]{:S(2)}) collective-permute-start(bf16[1,128,3072]{1,2,0:T(8,128)(2,1)S(1)} %get-tuple-element.124), channel_id=1, source_target_pairs={{0,16},{4,20},{8,24},{12,28},{16,0},{20,4},{24,8},{28,12},{1,17},{... | collective-permute-start | bytes 2359304 | tf_op jit(solution)/shard_map/ppermute | solution.py:423
  697.3 36.4 %collective-permute-start.37 = (bf16[1,128,3072]{1,2,0:T(8,128)(2,1)S(1)}, bf16[1,128,3072]{1,2,0:T(8,128)(2,1)S(1)}, u32[]{:S(2)}, u32[]{:S(2)}) collective-permute-start(bf16[1,128,3072]{1,2,0:T(8,128)(2,1)S(1)} %get-tuple-element.121), channel_id=1, source_target_pairs={{0,16},{4,20},{8,24},{12,28},{16,0},{20,4},{24,8},{28,12},{1,17},{... | collective-permute-start | bytes 2359304 | tf_op jit(solution)/shard_map/ppermute | solution.py:423
  698.7 36.2 %collective-permute-start.36 = (bf16[1,128,3072]{1,2,0:T(8,128)(2,1)S(1)}, bf16[1,128,3072]{1,2,0:T(8,128)(2,1)S(1)}, u32[]{:S(2)}, u32[]{:S(2)}) collective-permute-start(bf16[1,128,3072]{1,2,0:T(8,128)(2,1)S(1)} %get-tuple-element.119), channel_id=1, source_target_pairs={{0,8},{4,12},{8,0},{12,4},{16,24},{20,28},{24,16},{28,20},{1,9},{5... | collective-permute-start | bytes 2359304 | tf_op jit(solution)/shard_map/ppermute | solution.py:423
  717.5 33.7 %collective-permute-start.34 = (bf16[1,128,3072]{1,2,0:T(8,128)(2,1)S(1)}, bf16[1,128,3072]{1,2,0:T(8,128)(2,1)S(1)}, u32[]{:S(2)}, u32[]{:S(2)}) collective-permute-start(bf16[1,128,3072]{1,2,0:T(8,128)(2,1)S(1)} %get-tuple-element.117), channel_id=1, source_target_pairs={{0,24},{4,28},{8,16},{12,20},{16,8},{20,12},{24,0},{28,4},{1,25},{... | collective-permute-start | bytes 2359304 | tf_op jit(solution)/shard_map/ppermute | solution.py:423
  733.7 32.4 %collective-permute-start.33 = (bf16[1,128,3072]{1,2,0:T(8,128)(2,1)S(1)}, bf16[1,128,3072]{1,2,0:T(8,128)(2,1)S(1)}, u32[]{:S(2)}, u32[]{:S(2)}) collective-permute-start(bf16[1,128,3072]{1,2,0:T(8,128)(2,1)S(1)} %get-tuple-element.118), channel_id=1, source_target_pairs={{0,16},{4,20},{8,24},{12,28},{16,0},{20,4},{24,8},{28,12},{1,17},{... | collective-permute-start | bytes 2359304 | tf_op jit(solution)/shard_map/ppermute | solution.py:423
  773.2 50.2 %collective-permute-start.49 = (bf16[128,2816]{0,1:T(8,128)(2,1)S(1)}, bf16[128,2816]{0,1:T(8,128)(2,1)}, u32[]{:S(2)}, u32[]{:S(2)}) collective-permute-start(bf16[128,2816]{0,1:T(8,128)(2,1)S(1)} %get-tuple-element.114), channel_id=1, source_target_pairs={{0,3},{1,2},{2,1},{3,0},{4,7},{5,6},{6,5},{7,4},{8,11},{9,10},{10,... | collective-permute-start | bytes 2162696 | tf_op jit(solution)/shard_map/ppermute | solution.py:423
  775.4 61.9 %collective-permute-start.48 = (bf16[128,2816]{0,1:T(8,128)(2,1)S(1)}, bf16[128,2816]{0,1:T(8,128)(2,1)}, u32[]{:S(2)}, u32[]{:S(2)}) collective-permute-start(bf16[128,2816]{0,1:T(8,128)(2,1)S(1)} %get-tuple-element.115), channel_id=1, source_target_pairs={{0,2},{1,3},{2,0},{3,1},{4,6},{5,7},{6,4},{7,5},{8,10},{9,11},{10,... | collective-permute-start | bytes 2162696 | tf_op jit(solution)/shard_map/ppermute | solution.py:423
  777.4 60.0 %collective-permute-start.47 = (bf16[128,2816]{0,1:T(8,128)(2,1)S(1)}, bf16[128,2816]{0,1:T(8,128)(2,1)}, u32[]{:S(2)}, u32[]{:S(2)}) collective-permute-start(bf16[128,2816]{0,1:T(8,128)(2,1)S(1)} %get-tuple-element.113), channel_id=1, source_target_pairs={{0,1},{1,0},{2,3},{3,2},{4,5},{5,4},{6,7},{7,6},{8,9},{9,8},{10,11... | collective-permute-start | bytes 2162696 | tf_op jit(solution)/shard_map/ppermute | solution.py:423
  (160 other events, 1637.7 us)
Sparse Core Ops, SparseCore 0:
  10.9 89.8 all-gather.4
  104.2 85.4 all-gather.6
  193.2 76.7 all-gather.8
  273.2 76.8 all-gather.10
